TPU v7x, 32 devices: a whole 2x2x4 slice. The times are simulated.
32 devices in a mesh: row: 4 (over y, core), col: 8 (over z, x).
Axes of the slice: x: 2, y: 2, z: 4, core: 2. Of those that a mesh axis runs over, the one named last changes fastest.
Arguments:
- inverse: float32 [16384, 16384], P('row', 'col'), may hold values from -6 to 6
- front_blocks: int32 [2, 16], replicated, may hold values from 0 to 63, as said below
- panels: float32 [2, 4096, 256], P(None, 'row'), may hold values from -0.09375 to 0.09375
- diag_terms: float32 [2, 256, 256], replicated, may hold values from -6 to 6
- bounds: int32 [2, 4], replicated, may hold values from 1 to 128, 256 in all within a row
Outputs:
- border: float32 [2, 4096, 256], P(None, ('row', 'col'))
- diag_block: float32 [2, 256, 256], replicated
Inputs may be any that keep to these rules, and one draw needn't show every extreme that they name: `front_blocks`: each row names 16 distinct blocks. Positions 4 r to 4 r + 3 name blocks of four different groups of 16 consecutive blocks, and every such group is named at exactly four positions, of four different r. Positions 2 o and 2 o + 1 name blocks of two different groups of 8 consecutive blocks, and every such group is named at exactly two positions, of two different o.
All inputs are finite; a program needn't handle non-finite values.
Results may differ from a plain program's by a relative error of at most 0.0001.
Values sent between devices are 32-bit elements; how exact they have to be, the bound alone decides.
A program may use at most 128 MiB of HBM per device.

v0:
```python
import functools

import jax
import jax.numpy as jnp
from jax import lax
from jax.experimental import pallas as pl
from jax.experimental.pallas import tpu as pltpu
from jax.sharding import PartitionSpec as P

BS = 256


def split(a):
    hi = a.astype(jnp.bfloat16)
    lo = (a - hi.astype(jnp.float32)).astype(jnp.bfloat16)
    return hi, lo


def dot3(a, b):
    ah, al = a
    bh, bl = b
    dot = functools.partial(jnp.dot, preferred_element_type=jnp.float32)
    return dot(ah, bh) + (dot(ah, bl) + dot(al, bh))


def tile_kernel(dims, fb, inv, w, out, tiles, sem):
    fronts, kb, nr, nc, rg, cg, nz, nx = dims
    r = lax.axis_index("row")
    c = lax.axis_index("col")
    per_owner = kb // lax.axis_size("row")
    owners = []
    for f in range(fronts):
        rows = [jnp.int32(0)] * nr
        cols = [jnp.int32(0)] * nc
        own = [jnp.int32(0)] * nc
        n = jnp.int32(0)
        m = jnp.int32(0)
        for p in range(kb):
            b = fb[f, p]
            here = (b // rg) == r
            for i in range(nr):
                rows[i] = jnp.where(here & (n == i), b % rg, rows[i])
            n = n + here.astype(jnp.int32)
            there = (b // cg) == c
            for i in range(nc):
                hit = there & (m == i)
                cols[i] = jnp.where(hit, b % cg, cols[i])
                own[i] = jnp.where(hit, p // per_owner, own[i])
            m = m + there.astype(jnp.int32)
        owners.append(own)
        for k in range(nc):
            for i in range(nr):
                pltpu.make_async_copy(
                    inv.at[
                        pl.ds(pl.multiple_of(rows[i] * BS, BS), BS),
                        pl.ds(pl.multiple_of(cols[k] * BS, BS), BS),
                    ],
                    tiles.at[f, k, pl.ds(i * BS, BS)],
                    sem.at[f, k, i],
                ).start()
    sub = BS // (nz * nx)
    for f in range(fronts):
        total = None
        for k in range(nc):
            for i in range(nr):
                pltpu.make_async_copy(
                    inv.at[pl.ds(0, BS), pl.ds(0, BS)],
                    tiles.at[f, k, pl.ds(i * BS, BS)],
                    sem.at[f, k, i],
                ).wait()
            term = dot3(split(tiles[f, k]), split(w[owners[f][k], f]))
            total = term if total is None else total + term
        for i in range(nr):
            for s in range(nx):
                for z in range(nz):
                    at = i * BS + (s * nz + z) * sub
                    out[f, s, i, z] = total[at : at + sub]


MESH = pl.DeviceIdType.MESH


def greet(peers):
    barrier = pltpu.get_barrier_semaphore()
    for peer in peers:
        pl.semaphore_signal(barrier, inc=1, device_id=peer, device_id_type=MESH)
    pl.semaphore_wait(barrier, len(peers))


class Mail:
    def __init__(self, send_sem, recv_sem):
        self.send_sem, self.recv_sem = send_sem, recv_sem
        self.sent = []

    def send(self, src, dst, peer):
        at = len(self.sent)
        copy = pltpu.make_async_remote_copy(
            src_ref=src,
            dst_ref=dst,
            send_sem=self.send_sem.at[at],
            recv_sem=self.recv_sem.at[at],
            device_id=peer,
            device_id_type=MESH,
        )
        copy.start()
        self.sent.append(copy)
        return copy

    def close(self):
        for copy in self.sent:
            copy.wait_send()


def gather_kernel(dims, fb, panels, out, send_sem, recv_sem):
    fronts, n_row, cg, cuts = dims
    r = lax.axis_index("row")
    c = lax.axis_index("col")
    core, y, ny = lax.rem(r, 2), r // 2, n_row // 2
    partner = r + 1 - 2 * core
    lines = [lax.rem(y + d, ny) * 2 + core for d in range(1, ny)]
    greet([(partner, c)] + [(line, c) for line in lines])
    per_owner = panels.shape[1]
    mail = Mail(send_sem, recv_sem)
    height = BS // cuts
    arriving, relayed = [], []
    for f in range(fronts):
        at = jnp.int32(0)
        found = jnp.int32(0)
        for j in range(per_owner):
            hit = (fb[f, r * per_owner + j] // cg) == c
            at = jnp.where(hit, j, at)
            found = jnp.where(hit, 1, found)
        out[r, f] = jnp.where(found == 1, panels[f, at], 0.0)
        for h in range(cuts):
            rows = pl.ds(h * height, height)
            for d, line in enumerate(lines, 1):
                piece = out.at[r, f, rows]
                came = lax.rem(y + ny - d, ny) * 2 + core
                arriving.append((mail.send(piece, piece, (line, c)), came, f, rows))
        mine = out.at[r, f]
        relayed.append(mail.send(mine, mine, (partner, c)))
    for copy, came, f, rows in arriving:
        copy.wait_recv()
        piece = out.at[came, f, rows]
        relayed.append(mail.send(piece, piece, (partner, c)))
    for copy in relayed:
        copy.wait_recv()
    mail.close()


def copies_of(dims):
    fronts, kb, nr, nc, rg, cg, nz, nx = dims
    n_row, n_col = kb // nr, kb // nc
    total = nr * (nx - 1) + nr * (nz - 1) + (n_row - 1) + (nz - 1)
    return fronts * (total + 2 * (1 + n_row // 2 - 1 + n_col - 1))


def sum_kernel(dims, fb, partial, w, border, acc, xbuf, xs, zbuf, zs, slots, rbuf, qs, cbuf, ybuf, lbuf, red, send_sem, recv_sem):
    fronts, kb, nr, nc, rg, cg, nz, nx = dims
    n_row, n_col = kb // nr, kb // nc
    per_owner = kb // n_row
    r = lax.axis_index("row")
    c = lax.axis_index("col")
    s, z = lax.rem(c, nx), c // nx
    core, y, ny = lax.rem(r, 2), r // 2, n_row // 2
    partner = r + 1 - 2 * core
    other = 1 - core
    cols = [lax.rem(c + d, n_col) for d in range(1, n_col)]
    rows = [lax.rem(r + d, n_row) for d in range(1, n_row)]
    greet([(r, col) for col in cols] + [(row, c) for row in rows])
    mail = Mail(send_sem, recv_sem)
    width = w.shape[2]
    share = w.shape[1]
    part = acc.shape[4]
    sub = zs.shape[2]

    along_x = {}
    for f in range(fronts):
        for n in range(nr):
            for d in range(1, nx):
                to = lax.rem(s + d, nx)
                along_x[f, n, d] = mail.send(
                    partial.at[f, to, n], xbuf.at[f, n, d - 1], (r, z * nx + to)
                )

    along_z = {}

    def x_sum(f, n):
        for d in range(1, nx):
            along_x[f, n, d].wait_recv()
        total = partial[f, s, n]
        for d in range(1, nx):
            total = total + xbuf[f, n, d - 1]
        xs[f, n] = total
        for d in range(1, nz):
            to = lax.rem(z + d, nz)
            along_z[f, n, d] = mail.send(
                xs.at[f, n, to], zbuf.at[f, n, d - 1], (r, to * nx + s)
            )

    def z_sum(f, n):
        for d in range(1, nz):
            along_z[f, n, d].wait_recv()
        total = xs[f, n, z]
        for d in range(1, nz):
            total = total + zbuf[f, n, d - 1]
        zs[f, n] = total

    along_row = {}

    def row_send(f):
        if nr == n_row:
            source = zs
        else:
            source = slots
            n = jnp.int32(0)
            for row in range(n_row):
                named = jnp.int32(0)
                for j in range(per_owner):
                    named = jnp.where((fb[f, row * per_owner + j] // rg) == r, 1, named)
                slots[f, row] = jnp.where(named == 1, zs[f, jnp.minimum(n, nr - 1)], 0.0)
                n = n + named
        rbuf[f][r] = source[f, r]
        for d in range(1, n_row):
            to = rows[d - 1]
            along_row[f, d] = mail.send(source.at[f, to], rbuf[f].at[r], (to, c))

    along_owner = {}

    def owner_send(f):
        for d in range(1, n_row):
            along_row[f, d].wait_recv()
        for q in range(nz):
            qs[f, q] = rbuf[f][fb[f, r * per_owner + q] // rg]
        border[f, z] = qs[f, z]
        for d in range(1, nz):
            to = lax.rem(z + d, nz)
            along_owner[f, d] = mail.send(qs.at[f, to], border.at[f, z], (r, to * nx + s))

    to_core = {}

    def product(f):
        for d in range(1, nz):
            along_owner[f, d].wait_recv()
        wh, wl = split(w[f])
        ph, plo = split(jnp.concatenate([border[f, q] for q in range(nz)], axis=0))
        dot = functools.partial(
            lax.dot_general,
            dimension_numbers=(((0,), (0,)), ((), ())),
            preferred_element_type=jnp.float32,
        )
        total = dot(wh, ph) + (dot(wh, plo) + dot(wl, ph))
        for a in range(2):
            for b in range(ny):
                for e in range(n_col):
                    at = ((a * ny + b) * n_col + e) * part
                    red[f, a, b, e] = total[at : at + part]
        to_core[f] = mail.send(red.at[f, other], cbuf.at[f], (partner, c))

    to_y = {}

    def core_sum(f):
        to_core[f].wait_recv()
        red[f, core] = red[f, core] + cbuf[f]
        for d in range(1, ny):
            to = lax.rem(y + d, ny)
            to_y[f, d] = mail.send(
                red.at[f, core, to], ybuf.at[f, d - 1], (to * 2 + core, c)
            )

    to_col = {}

    def y_sum(f):
        for d in range(1, ny):
            to_y[f, d].wait_recv()
        total = red[f, core, y]
        for d in range(1, ny):
            total = total + ybuf[f, d - 1]
        red[f, core, y] = total
        for d in range(1, n_col):
            to = cols[d - 1]
            to_col[f, d] = mail.send(red.at[f, core, y, to], lbuf.at[f, d - 1], (r, to))

    back_col = {}

    def col_sum(f):
        for d in range(1, n_col):
            to_col[f, d].wait_recv()
        total = red[f, core, y, c]
        for d in range(1, n_col):
            total = total + lbuf[f, d - 1]
        acc[f, core, y, c] = total
        mine = acc.at[f, core, y, c]
        for d in range(1, n_col):
            back_col[f, d] = mail.send(mine, mine, (r, cols[d - 1]))

    back_y = {}

    def y_back(f):
        for d in range(1, n_col):
            back_col[f, d].wait_recv()
        mine = acc.at[f, core, y]
        for d in range(1, ny):
            to = lax.rem(y + d, ny)
            back_y[f, d] = mail.send(mine, mine, (to * 2 + core, c))

    back_core = {}

    def core_back(f):
        for d in range(1, ny):
            back_y[f, d].wait_recv()
        mine = acc.at[f, core]
        back_core[f] = mail.send(mine, mine, (partner, c))

    def finish(f):
        back_core[f].wait_recv()

    for n in range(nr):
        x_sum(0, n)
    for f in range(fronts):
        for n in range(nr):
            if f + 1 < fronts:
                x_sum(f + 1, n)
            z_sum(f, n)
            if f > 0 and n == nr // 2 - 1:
                owner_send(f - 1)
        row_send(f)
        if f > 0:
            product(f - 1)
    last = fronts - 1
    owner_send(last)
    for f in range(last):
        core_sum(f)
    product(last)
    for f in range(last):
        y_sum(f)
    core_sum(last)
    for f in range(last):
        col_sum(f)
    y_sum(last)
    for f in range(last):
        y_back(f)
    col_sum(last)
    for f in range(last):
        core_back(f)
    y_back(last)
    core_back(last)
    for f in range(fronts):
        finish(f)
    mail.close()


def body(inverse, front_blocks, panels, diag_terms, bounds):
    n_row = lax.axis_size("row")
    n_col = lax.axis_size("col")
    r = lax.axis_index("row")
    c = lax.axis_index("col")
    rows_loc, cols_loc = inverse.shape
    rg = rows_loc // BS
    cg = cols_loc // BS
    fronts, kb = front_blocks.shape
    width = panels.shape[2]
    per_owner = kb // n_row
    nr = kb // n_row
    nc = kb // n_col
    nz = per_owner
    nx = n_col // nz
    sub = BS // n_col
    share = nz * sub

    cuts = 2
    gdims = (fronts, n_row, cg, cuts)
    count = fronts * (cuts * 2 * (n_row // 2 - 1) + 1)
    vmem = pl.BlockSpec(memory_space=pltpu.VMEM)
    smem = pl.BlockSpec(memory_space=pltpu.SMEM)
    gathered = pl.pallas_call(
        functools.partial(gather_kernel, gdims),
        out_shape=jax.ShapeDtypeStruct((n_row, fronts, BS, width), jnp.float32),
        in_specs=[smem, vmem],
        out_specs=vmem,
        scratch_shapes=[pltpu.SemaphoreType.DMA((count,))] * 2,
        compiler_params=pltpu.CompilerParams(
            collective_id=0, has_side_effects=True, vmem_limit_bytes=24 << 20
        ),
    )(front_blocks, panels.reshape(fronts, per_owner, BS, width))

    dims = (fronts, kb, nr, nc, rg, cg, nz, nx)
    partial = pl.pallas_call(
        functools.partial(tile_kernel, dims),
        out_shape=jax.ShapeDtypeStruct((fronts, nx, nr, nz, sub, width), jnp.float32),
        in_specs=[
            pl.BlockSpec(memory_space=pltpu.SMEM),
            pl.BlockSpec(memory_space=pl.ANY),
            pl.BlockSpec(memory_space=pltpu.VMEM),
        ],
        out_specs=pl.BlockSpec(memory_space=pltpu.VMEM),
        scratch_shapes=[
            pltpu.VMEM((fronts, nc, nr * BS, BS), jnp.float32),
            pltpu.SemaphoreType.DMA((fronts, nc, nr)),
        ],
        compiler_params=pltpu.CompilerParams(vmem_limit_bytes=40 << 20),
    )(front_blocks, inverse, gathered)

    w_mine = lax.dynamic_slice_in_dim(panels, c * share, share, 1)
    ny = n_row // 2
    part = width // (n_row * n_col)
    count = copies_of(dims)
    f32 = jnp.float32
    border, acc = pl.pallas_call(
        functools.partial(sum_kernel, dims),
        out_shape=(
            jax.ShapeDtypeStruct((fronts, nz, sub, width), f32),
            jax.ShapeDtypeStruct((fronts, 2, ny, n_col, part, width), f32),
        ),
        in_specs=[smem, vmem, vmem],
        out_specs=(vmem, vmem),
        scratch_shapes=[
            pltpu.VMEM((fronts, nr, nx - 1, nz, sub, width), f32),
            pltpu.VMEM((fronts, nr, nz, sub, width), f32),
            pltpu.VMEM((fronts, nr, nz - 1, sub, width), f32),
            pltpu.VMEM((fronts, nr, sub, width), f32),
            pltpu.VMEM((fronts, n_row, sub, width), f32),
            [pltpu.VMEM((n_row, sub, width), f32)] * fronts,
            pltpu.VMEM((fronts, nz, sub, width), f32),
            pltpu.VMEM((fronts, ny, n_col, part, width), f32),
            pltpu.VMEM((fronts, ny - 1, n_col, part, width), f32),
            pltpu.VMEM((fronts, n_col - 1, part, width), f32),
            pltpu.VMEM((fronts, 2, ny, n_col, part, width), f32),
            pltpu.SemaphoreType.DMA((count,)),
            pltpu.SemaphoreType.DMA((count,)),
        ],
        compiler_params=pltpu.CompilerParams(
            collective_id=1, has_side_effects=True, vmem_limit_bytes=40 << 20
        ),
    )(front_blocks, partial, w_mine)
    product = border.reshape(fronts, share, width)
    summed = acc.reshape(fronts, width, width)
    ends = jnp.cumsum(bounds, axis=1)
    columns = jnp.arange(width, dtype=jnp.int32)
    ids = jnp.sum((columns[None, :, None] >= ends[:, None, :]).astype(jnp.int32), axis=2)
    same = (ids[:, :, None] == ids[:, None, :]).astype(jnp.float32)
    return (-product, same * (diag_terms + summed))


def solution(mesh):
    placed = (P("row", "col"), P(), P(None, "row", None), P(), P())
    return jax.shard_map(
        body,
        mesh=mesh,
        in_specs=placed,
        out_specs=(P(None, ("row", "col"), None), P()),
        check_vma=False,
    )
```

profile of v0, /device:TPU:0, one launch (start us, length us, event | category | flops | bytes accessed | tf_op | source)
XLA Modules:
  0.0 90.7 jit_solution(671706383263313529)
XLA Ops:
  0.6 0.0 copy-start
  0.6 1.6 %copy-done = f32[2,1024,256]{2,1,0:T(8,128)S(1)} copy-done((f32[2,1024,256]{2,1,0:T(8,128)S(1)}, f32[2,1024,256]{2,1,0:T(8,128)}, u32[]{:S(2)}) %copy-start) | copy-done | bytes 2097176
  2.2 0.0 copy-start.1
  2.2 0.7 copy-done.1
  2.9 0.0 copy-start.2
  2.9 17.4 %shard_map.68.w = f32[4,2,256,256]{3,2,1,0:T(8,128)S(1)} custom-call(s32[2,16]{1,0:T(2,128)S(1)} %copy-done.1, f32[2,4,256,256]{3,2,1,0:T(8,128)S(1)} %bitcast.6), custom_call_target="tpu_custom_call" | custom-call | tf_op jit(solution)/shard_map/pallas_call | solution.py:376
  20.3 0.0 copy-done.2
  20.3 5.8 %shard_map.69.partial = f32[2,2,4,4,32,256]{5,4,3,2,1,0:T(8,128)S(1)} custom-call(s32[2,16]{1,0:T(2,128)S(1)} %copy-done.2, f32[4096,2048]{1,0:T(8,128)} %inv.1, f32[4,2,256,256]{3,2,1,0:T(8,128)S(1)} %shard_map.68.w), custom_call_target="tpu_custom_call" | custom-call | tf_op jit(solution)/shard_map/pallas_call | solution.py:388
  26.1 0.0 copy-start.4
  26.1 0.0 copy-start.3
  26.1 1.0 %constant_dynamic-slice_fusion.w = f32[2,128,256]{2,1,0:T(8,128)S(1)} fusion(f32[2,1024,256]{2,1,0:T(8,128)} %param.7, s32[]{:T(128)S(6)} %select_n.3), kind=kLoop, calls=%fused_computation.4 | loop fusion | bytes 524292 | tf_op jit(solution)/shard_map/dynamic_slice | solution.py:404
  27.2 61.6 %shard_map.70 = (f32[2,4,32,256]{3,2,1,0:T(8,128)S(1)}, f32[2,2,2,8,8,256]{5,4,3,2,1,0:T(8,128)S(1)}) custom-call(s32[2,16]{1,0:T(2,128)S(1)} %copy-done.2, f32[2,2,4,4,32,256]{5,4,3,2,1,0:T(8,128)S(1)} %shard_map.69.partial, f32[2,128,256]{2,1,0:T(8,128)S(1)} %constant_dynamic-slice_fusion.w), custom_call_target="tpu_custom_call" | custom-call | tf_op jit(solution)/shard_map/pallas_call | solution.py:409
  88.7 0.7 neg.6
  89.5 0.0 copy-done.4
  89.5 0.2 reduce_window_sum.11
  89.6 0.1 convert_reduce_fusion
  89.7 0.0 copy-done.3
  89.7 0.9 %fusion = f32[2,256,256]{2,1,0:T(8,128)} fusion(f32[2,256,256]{2,1,0:T(8,128)S(1)} %copy-done.3, f32[2,2,2,8,8,256]{5,4,3,2,1,0:T(8,128)S(1)} %get-tuple-element.5, s32[2,256]{1,0:T(2,128)S(1)} %convert_reduce_fusion), kind=kLoop, calls=%fused_computation.1 | loop fusion | flops 393216 | bytes 1574912 | tf_op jit(solution)/shard_map/mul | solution.py:442
Async XLA Ops:
  0.6 1.6 %copy-start = (f32[2,1024,256]{2,1,0:T(8,128)S(1)}, f32[2,1024,256]{2,1,0:T(8,128)}, u32[]{:S(2)}) copy-start(f32[2,1024,256]{2,1,0:T(8,128)} %param.7) | copy-start | bytes 6291460
  2.2 0.7 copy-start.1
  2.9 17.4 %copy-start.2 = (s32[2,16]{1,0:T(2,128)S(1)}, s32[2,16]{1,0:T(2,128)}, u32[]{:S(2)}) copy-start(s32[2,16]{1,0:T(2,128)} %fb.5) | copy-start | bytes 388
  26.1 63.4 %copy-start.4 = (s32[2,4]{1,0:T(2,128)S(1)}, s32[2,4]{1,0:T(2,128)}, u32[]{:S(2)}) copy-start(s32[2,4]{1,0:T(2,128)} %param.9) | copy-start | bytes 100
  26.1 63.6 %copy-start.3 = (f32[2,256,256]{2,1,0:T(8,128)S(1)}, f32[2,256,256]{2,1,0:T(8,128)}, u32[]{:S(2)}) copy-start(f32[2,256,256]{2,1,0:T(8,128)} %param.8) | copy-start | bytes 1572868
where the time goes:
time: 90.9 us; the launch traced here: 90.7 us
  Pallas kernels  84.7 us (93%)
  local copies, waits for them, and re-layouts  3.31 us (4%)
  other arithmetic  1.93 us (2%)
    pallas_call x1, Pallas kernels, body(): pl.pallas_call(functools.partial(sum_kernel, dims), out_shape=(jax.ShapeD...  61.6 us
    pallas_call x1, Pallas kernels, body(): pl.pallas_call(functools.partial(gather_kernel, gdims), out_shape=jax.Sha...  17.4 us
    pallas_call x1, Pallas kernels, body(): pl.pallas_call(functools.partial(tile_kernel, dims), out_shape=jax.ShapeD...  5.8 us
    unnamed x10, local copies, waits for them, and re-layouts  2.28 us

commit v1 on v0

v1 whole, which is shorter than its diff:
```python
import functools

import jax
import jax.numpy as jnp
from jax import lax
from jax.experimental import pallas as pl
from jax.experimental.pallas import tpu as pltpu
from jax.sharding import PartitionSpec as P

BS = 256
MESH = pl.DeviceIdType.MESH


def split(a):
    hi = a.astype(jnp.bfloat16)
    lo = (a - hi.astype(jnp.float32)).astype(jnp.bfloat16)
    return hi, lo


def dot(a, b):
    return jnp.dot(a, b, preferred_element_type=jnp.float32)


def fetch_kernel(dims, fb_hbm, inv, panels, tiles, wsel, fb, fb_sem, sem, wsem):
    fronts, kb, n_row, n_col, nz, nx, rg, cg, nh, hw = dims
    r = lax.axis_index("row")
    c = lax.axis_index("col")
    per_owner = kb // n_row
    nc = kb // n_col
    table = pltpu.make_async_copy(fb_hbm, fb, fb_sem)
    table.start()
    table.wait()
    copies = []
    for f in range(fronts):
        at = jnp.int32(0)
        for j in range(per_owner):
            at = jnp.where(fb[f, r * per_owner + j] // cg == c, j, at)
        for h in range(nh):
            copies.append(
                pltpu.make_async_copy(
                    panels.at[f, at, :, pl.ds(h * hw, hw)], wsel.at[f, h], wsem.at[f, h]
                )
            )
            copies[-1].start()
        cols = [jnp.int32(0)] * nc
        m = jnp.int32(0)
        rows = [jnp.int32(0)] * n_row
        for p in range(kb):
            b = fb[f, p]
            there = b // cg == c
            for k in range(nc):
                cols[k] = jnp.where(there & (m == k), b % cg, cols[k])
            m = m + there.astype(jnp.int32)
            t = p // per_owner
            rows[t] = jnp.where(b // rg == r, b % rg, rows[t])
        for t in range(n_row):
            for k in range(nc):
                copies.append(
                    pltpu.make_async_copy(
                        inv.at[
                            pl.ds(pl.multiple_of(rows[t] * BS, BS), BS),
                            pl.ds(pl.multiple_of(cols[k] * BS, BS), BS),
                        ],
                        tiles.at[f, t, :, pl.ds(k * BS, BS)],
                        sem.at[f, t, k],
                    )
                )
                copies[-1].start()
    for copy in copies:
        copy.wait()


class Mail:
    def __init__(self, send_sem, recv_sem):
        self.send_sem, self.recv_sem = send_sem, recv_sem
        self.sent = []

    def send(self, src, dst, peer):
        at = len(self.sent)
        copy = pltpu.make_async_remote_copy(
            src_ref=src,
            dst_ref=dst,
            send_sem=self.send_sem.at[at],
            recv_sem=self.recv_sem.at[at],
            device_id=peer,
            device_id_type=MESH,
        )
        copy.start()
        self.sent.append(copy)
        return copy

    def close(self):
        for copy in self.sent:
            copy.wait_send()


CUTS = 2
AHEAD = 4


def copies_of(dims):
    fronts, kb, n_row, n_col, nz, nx, rg, cg, nh, hw = dims
    gather = 2 * CUTS * (n_row // 2 - 1) + 1
    sums = n_row * (nx - 1) + (n_row - 1) + (nz - 1)
    diag = 2 * (n_row * nx - 1) + (nz - 1)
    return fronts * nh * (gather + sums + diag)


def node_ids(bounds, f, first, shape, dim):
    at = lax.broadcasted_iota(jnp.int32, shape, dim) + first
    ids = jnp.zeros(shape, jnp.int32)
    end = jnp.int32(0)
    for s in range(bounds.shape[1]):
        end = end + bounds[f, s]
        ids = ids + (at >= end).astype(jnp.int32)
    return ids


def main_kernel(
    dims, fb_hbm, bounds_hbm, tiles, wsel, panels, bsum, pkall,
    fb, bounds, th, tl, bm, wb, part, xbuf, xs, rbuf, qs, zbuf, pan, pth, ptl,
    dpk, rsb, zb, local_sem, send_sem, recv_sem,
):
    fronts, kb, n_row, n_col, nz, nx, rg, cg, nh, hw = dims
    r = lax.axis_index("row")
    c = lax.axis_index("col")
    s, z = lax.rem(c, nx), c // nx
    core, y, ny = lax.rem(r, 2), r // 2, n_row // 2
    per_owner = kb // n_row
    nc = kb // n_col
    share = BS // nx
    chunks = fronts * nh
    groups = n_row * nx
    half = dpk.shape[1] * dpk.shape[2]
    rows_each = dpk.shape[2]
    total_pieces = chunks * n_row

    def row_at(dy, dk):
        return lax.rem(y + dy, ny) * 2 + lax.rem(core + dk, 2)

    offsets = [(dy, dk) for dy in range(1, ny) for dk in range(2)] + [(0, 1), (0, 0)]
    slots = [row_at(dy, dk) for dy, dk in offsets]
    partner = row_at(0, 1)
    mine = r * nx + s
    plane = []
    for dy, dk in offsets:
        for ds in range(nx):
            if (dy, dk, ds) != (0, 0, 0):
                row, x = row_at(dy, dk), lax.rem(s + ds, nx)
                plane.append((row * nx + x, (row, z * nx + x)))
    depth = [lax.rem(z + d, nz) for d in range(1, nz)]

    small = [
        pltpu.make_async_copy(fb_hbm, fb, local_sem.at[0]),
        pltpu.make_async_copy(bounds_hbm, bounds, local_sem.at[1]),
    ]
    for copy in small:
        copy.start()
    own_rows = []
    for f in range(fronts):
        for j in range(nz):
            at = len(own_rows)
            copy = pltpu.make_async_copy(
                panels.at[f, j, pl.ds(pl.multiple_of(s * share, share), share), :],
                pan.at[f, j],
                local_sem.at[2 + at],
            )
            copy.start()
            own_rows.append(copy)

    barrier = pltpu.get_barrier_semaphore()
    peers = [peer for _, peer in plane] + [(r, to * nx + s) for to in depth]
    for peer in peers:
        pl.semaphore_signal(barrier, inc=1, device_id=peer, device_id_type=MESH)
    pl.semaphore_wait(barrier, len(peers))
    mail = Mail(send_sem, recv_sem)
    height = BS // CUTS
    line, beside, relayed = {}, {}, {}

    def w_send(i):
        f, h = divmod(i, nh)
        line[i] = []
        for cut in range(CUTS):
            rows = pl.ds(cut * height, height)
            for d in range(1, ny):
                copy = mail.send(wsel.at[f, h, rows], wb[i].at[r, rows], (row_at(d, 0), c))
                line[i].append((copy, row_at(ny - d, 0), rows))
        beside[i] = mail.send(wsel.at[f, h], wb[i].at[r], (partner, c))
        wb[i][r] = wsel[f, h]

    def w_relay(i):
        relayed[i] = []
        for copy, came, rows in line[i]:
            copy.wait_recv()
            piece = wb[i].at[came, rows]
            relayed[i].append(mail.send(piece, piece, (partner, c)))

    def w_ready(i):
        f = i // nh
        beside[i].wait_recv()
        for copy in relayed[i]:
            copy.wait_recv()
        own = [jnp.int32(0)] * nc
        m = jnp.int32(0)
        for p in range(kb):
            there = fb[f, p] // cg == c
            for k in range(nc):
                own[k] = jnp.where(there & (m == k), p // per_owner, own[k])
            m = m + there.astype(jnp.int32)
        for k in range(nc):
            hi, lo = split(wb[i][own[k]])
            bm[i, k * BS : (k + 1) * BS, :hw] = hi
            bm[i, k * BS : (k + 1) * BS, hw:] = lo

    def split_tiles(f):
        for t in range(n_row):
            hi, lo = split(tiles[f, t])
            th[f, t] = hi
            tl[f, t] = lo

    def split_panels(f):
        for j in range(nz):
            hi, lo = split(pan[f, j].T)
            pth[f, :, j * share : (j + 1) * share] = hi
            ptl[f, :, j * share : (j + 1) * share] = lo

    along_x, along_row, along_z = {}, {}, {}

    def piece_product(n):
        i, o = divmod(n, n_row)
        f = i // nh
        t = slots[o]
        both = dot(th[f, t], bm[i])
        low = dot(tl[f, t], bm[i, :, :hw])
        total = both[:, :hw] + (both[:, hw:] + low)
        for to in range(nx):
            part[i, o, to] = total[to * share : (to + 1) * share]
        for d in range(1, nx):
            to = lax.rem(s + d, nx)
            along_x[n, d] = mail.send(
                part.at[i, o, to], xbuf.at[i, o, d - 1], (r, z * nx + to)
            )

    def piece_sum(n):
        i, o = divmod(n, n_row)
        for d in range(1, nx):
            along_x[n, d].wait_recv()
        total = part[i, o, s]
        for d in range(1, nx):
            total = total + xbuf[i, o, d - 1]
        if o == n_row - 1:
            rbuf[i][r] = total
        else:
            xs[i, o] = total
            along_row[i, o] = mail.send(xs.at[i, o], rbuf[i].at[r], (slots[o], c))

    to_plane, to_depth, back = {}, {}, {}

    def z_stage(i):
        f, h = divmod(i, nh)
        for o in range(n_row - 1):
            along_row[i, o].wait_recv()
        for j in range(nz):
            qs[i, j] = rbuf[i][fb[f, r * per_owner + j] // rg]
        whole = jnp.concatenate([qs[i, j] for j in range(nz)], axis=0)
        hi, lo = split(whole)
        both = dot(pth[f], jnp.concatenate([hi, lo], axis=1))
        inner = both[:, :hw] + (both[:, hw:] + dot(ptl[f], hi))
        ids = node_ids(bounds, f, 0, (half, hw), 0)
        same = ids == node_ids(bounds, f, h * hw, (half, hw), 1)
        packed = jnp.where(same, inner[:half], inner[half:])
        for e in range(groups):
            dpk[i, e] = packed[e * rows_each : (e + 1) * rows_each]
        for at, (e, peer) in enumerate(plane):
            to_plane[i, at] = mail.send(dpk.at[i, e], rsb.at[i, at], peer)
        for d, to in enumerate(depth, 1):
            along_z[i, d] = mail.send(qs.at[i, to], zbuf.at[i, d - 1], (r, to * nx + s))

    def diag_sum(i):
        total = dpk[i, mine]
        for at in range(len(plane)):
            to_plane[i, at].wait_recv()
            total = total + rsb[i, at]
        zb[i, z] = total
        for d, to in enumerate(depth, 1):
            piece = zb.at[i, z]
            to_depth[i, d] = mail.send(piece, piece, (r, to * nx + s))

    def diag_back(i):
        for d in range(1, nz):
            to_depth[i, d].wait_recv()
        total = zb[i, 0]
        for j in range(1, nz):
            total = total + zb[i, j]
        pkall[i, mine] = total
        for at, (_, peer) in enumerate(plane):
            piece = pkall.at[i, mine]
            back[i, at] = mail.send(piece, piece, peer)

    def finish(i):
        f, h = divmod(i, nh)
        total = qs[i, z]
        for d in range(1, nz):
            along_z[i, d].wait_recv()
            total = total + zbuf[i, d - 1]
        bsum[f, :, h * hw : (h + 1) * hw] = total

    def done(i):
        for at in range(len(plane)):
            back[i, at].wait_recv()

    w_send(0)
    w_send(1)
    split_tiles(0)
    for copy in small:
        copy.wait()
    w_relay(0)
    w_ready(0)
    for n in range(AHEAD):
        piece_product(n)
    w_relay(1)
    for i in range(2, chunks):
        w_send(i)
    for copy in own_rows:
        copy.wait()
    for f in range(1, fronts):
        split_tiles(f)
    for f in range(fronts):
        split_panels(f)

    tasks = {}

    def plan(n, task, i):
        tasks.setdefault(min(n, total_pieces - 1), []).append((task, i))

    for i in range(chunks - 1):
        last = (i + 1) * n_row - 1
        plan(last + 2, z_stage, i)
        plan(last + 4, diag_sum, i)
        plan(last + 5, finish, i)
        plan(last + 6, diag_back, i)
    for n in range(total_pieces):
        piece_sum(n)
        ahead = n + AHEAD
        if ahead < total_pieces:
            if ahead % n_row == 0:
                w_ready(ahead // n_row)
            piece_product(ahead)
        if n % 2 == 1 and 2 + n // 2 < chunks:
            w_relay(2 + n // 2)
        if n < total_pieces - 1:
            for task, i in tasks.get(n, []):
                task(i)
    last = chunks - 1
    z_stage(last)
    for task, i in tasks.get(total_pieces - 1, []):
        task(i)
    diag_sum(last)
    diag_back(last)
    finish(last)
    for i in range(chunks):
        done(i)
    mail.close()


def last_kernel(bounds, bsum, pk, terms, border, diag):
    fronts, width = terms.shape[:2]
    half, hw = pk.shape[1:]
    border[...] = -bsum[...]
    for f in range(fronts):
        for h in range(width // hw):
            cols = node_ids(bounds, f, h * hw, (half, hw), 1)
            for a in range(width // half):
                same = (node_ids(bounds, f, a * half, (half, hw), 0) == cols).astype(jnp.float32)
                at = (f, pl.ds(a * half, half), pl.ds(h * hw, hw))
                diag[at] = same * (terms[at] + pk[f * (width // hw) + h])


def body(inverse, front_blocks, panels, diag_terms, bounds):
    n_row = lax.axis_size("row")
    n_col = lax.axis_size("col")
    rows_loc, cols_loc = inverse.shape
    rg = rows_loc // BS
    cg = cols_loc // BS
    fronts, kb = front_blocks.shape
    width = panels.shape[2]
    per_owner = kb // n_row
    nc = kb // n_col
    nz = per_owner
    nx = n_col // nz
    share = BS // nx
    nh = 2
    hw = width // nh
    half = width // 2
    chunks = fronts * nh
    groups = n_row * nx
    rows_each = half // groups
    dims = (fronts, kb, n_row, n_col, nz, nx, rg, cg, nh, hw)
    f32, bf16 = jnp.float32, jnp.bfloat16
    vmem = pl.BlockSpec(memory_space=pltpu.VMEM)
    smem = pl.BlockSpec(memory_space=pltpu.SMEM)
    anywhere = pl.BlockSpec(memory_space=pl.ANY)
    blocks = panels.reshape(fronts, per_owner, BS, width)

    tiles, wsel = pl.pallas_call(
        functools.partial(fetch_kernel, dims),
        out_shape=(
            jax.ShapeDtypeStruct((fronts, n_row, BS, nc * BS), f32),
            jax.ShapeDtypeStruct((fronts, nh, BS, hw), f32),
        ),
        in_specs=[anywhere, anywhere, anywhere],
        out_specs=(vmem, vmem),
        scratch_shapes=[
            pltpu.SMEM((fronts, kb), jnp.int32),
            pltpu.SemaphoreType.DMA(()),
            pltpu.SemaphoreType.DMA((fronts, n_row, nc)),
            pltpu.SemaphoreType.DMA((fronts, nh)),
        ],
        compiler_params=pltpu.CompilerParams(vmem_limit_bytes=24 << 20),
    )(front_blocks, inverse, blocks)

    count = copies_of(dims)
    V = pltpu.VMEM
    bsum, pk = pl.pallas_call(
        functools.partial(main_kernel, dims),
        out_shape=(
            jax.ShapeDtypeStruct((fronts, share, width), f32),
            jax.ShapeDtypeStruct((chunks, groups, rows_each, hw), f32),
        ),
        in_specs=[anywhere, anywhere, vmem, vmem, anywhere],
        out_specs=(vmem, vmem),
        scratch_shapes=[
            pltpu.SMEM((fronts, kb), jnp.int32),
            pltpu.SMEM(bounds.shape, jnp.int32),
            V((fronts, n_row, BS, nc * BS), bf16),
            V((fronts, n_row, BS, nc * BS), bf16),
            V((chunks, nc * BS, 2 * hw), bf16),
            [V((n_row, BS, hw), f32)] * chunks,
            V((chunks, n_row, nx, share, hw), f32),
            V((chunks, n_row, nx - 1, share, hw), f32),
            V((chunks, n_row, share, hw), f32),
            [V((n_row, share, hw), f32)] * chunks,
            V((chunks, nz, share, hw), f32),
            V((chunks, nz - 1, share, hw), f32),
            V((fronts, nz, share, width), f32),
            V((fronts, width, nz * share), bf16),
            V((fronts, width, nz * share), bf16),
            V((chunks, groups, rows_each, hw), f32),
            V((chunks, groups - 1, rows_each, hw), f32),
            V((chunks, nz, rows_each, hw), f32),
            pltpu.SemaphoreType.DMA((2 + fronts * nz,)),
            pltpu.SemaphoreType.DMA((count,)),
            pltpu.SemaphoreType.DMA((count,)),
        ],
        compiler_params=pltpu.CompilerParams(
            collective_id=0, has_side_effects=True, vmem_limit_bytes=48 << 20
        ),
    )(front_blocks, bounds, tiles, wsel, blocks)

    return pl.pallas_call(
        last_kernel,
        out_shape=(
            jax.ShapeDtypeStruct((fronts, share, width), f32),
            jax.ShapeDtypeStruct((fronts, width, width), f32),
        ),
        in_specs=[smem, vmem, vmem, vmem],
        out_specs=(vmem, vmem),
        compiler_params=pltpu.CompilerParams(vmem_limit_bytes=16 << 20),
    )(bounds, bsum, pk.reshape(chunks, half, hw), diag_terms)


def solution(mesh):
    placed = (P("row", "col"), P(), P(None, "row", None), P(), P())
    return jax.shard_map(
        body,
        mesh=mesh,
        in_specs=placed,
        out_specs=(P(None, ("row", "col"), None), P()),
        check_vma=False,
    )
```

time: 90.9 us -> 77.2 us (0.85)
  Pallas kernels: 84.7 us -> 72.2 us
  other arithmetic: 1.93 us -> 0 us
    pallas_call x3, Pallas kernels: 84.7 us -> 72.2 us  [the longest x1 67.3 us: body(): pl.pallas_call(functools.partial(main_kernel, dims), out_shape=(jax.Shape...]
    unnamed x10 -> x14, local copies, waits for them, and re-layouts: 2.28 us -> 4.21 us
    dynamic_slice x1 -> x0, local copies, waits for them, and re-layouts: 1.03 us -> none  [body(): w_mine = lax.dynamic_slice_in_dim(panels, c * share, share, 1)]
    mul x1 -> x0, other arithmetic: 0.94 us -> none  [body(): return (-product, same * (diag_terms + summed))]
where the time goes in v1:
time: 77.2 us; the launch traced here: 77.1 us
  Pallas kernels  72.2 us (94%)
  local copies, waits for them, and re-layouts  4.21 us (5%)
    pallas_call x1, Pallas kernels, body(): pl.pallas_call(functools.partial(main_kernel, dims), out_shape=(jax.Shape...  67.3 us
    unnamed x14, local copies, waits for them, and re-layouts  4.21 us
    pallas_call x1, Pallas kernels, body(): pl.pallas_call(functools.partial(fetch_kernel, dims), out_shape=(jax.Shap...  3.22 us
    pallas_call x1, Pallas kernels, body(): pl.pallas_call(last_kernel, out_shape=(jax.ShapeDtypeStruct((fronts, shar...  1.64 us

profile of v1, /device:TPU:0, one launch (start us, length us, event | category | flops | bytes accessed | tf_op | source)
XLA Modules:
  0.0 77.1 jit_solution(5061391029293772867)
XLA Ops:
  0.6 0.0 copy-start
  0.6 1.6 %copy-done = f32[2,1024,256]{2,1,0:T(8,128)S(1)} copy-done((f32[2,1024,256]{2,1,0:T(8,128)S(1)}, f32[2,1024,256]{2,1,0:T(8,128)}, u32[]{:S(2)}) %copy-start) | copy-done | bytes 2097176
  2.2 0.0 copy-start.4
  2.2 0.7 copy-done.4
  2.9 0.0 copy-start.1
  2.9 0.0 copy-start.5
  2.9 0.0 copy-start.6
  2.9 3.2 %shard_map.68 = (f32[2,4,256,512]{3,2,1,0:T(8,128)S(1)}, f32[2,2,256,128]{3,2,1,0:T(8,128)S(1)}) custom-call(s32[2,16]{1,0:T(2,128)S(1)} %copy-done.4, f32[4096,2048]{1,0:T(8,128)} %inv.1, f32[2,4,256,256]{3,2,1,0:T(8,128)S(1)} %bitcast.2), custom_call_target="tpu_custom_call" | custom-call | tf_op jit(solution)/shard_map/pallas_call | solution.py:405
  6.1 0.0 copy-start.2
  6.2 1.9 %copy-done.2 = f32[2,4,256,512]{3,2,1,0:T(8,128)} copy-done((f32[2,4,256,512]{3,2,1,0:T(8,128)}, f32[2,4,256,512]{3,2,1,0:T(8,128)S(1)}, u32[]{:S(2)}) %copy-start.2) | copy-done | bytes 4194328
  8.1 0.0 copy-start.3
  8.1 0.0 copy-done.1
  8.1 0.0 copy-done.5
  8.1 0.0 copy-done.6
  8.1 67.3 %shard_map.69 = (f32[2,128,256]{2,1,0:T(8,128)S(1)}, f32[4,8,16,128]{3,2,1,0:T(8,128)S(1)}) custom-call(s32[2,16]{1,0:T(2,128)S(1)} %copy-done.5, s32[2,4]{1,0:T(2,128)S(1)} %copy-done.6, f32[2,4,256,512]{3,2,1,0:T(8,128)} %copy-done.2, f32[2,2,256,128]{3,2,1,0:T(8,128)S(1)} %get-tuple-element.7.wsel, f32[2,4,256,256]{3,2,1,0:T(8,128)S(1)} %bitcast.3), custom_call_target="tpu_custom_call" | custom-call | tf_op jit(solution)/shard_map/pallas_call | solution.py:424
  75.4 0.0 copy-done.3
  75.4 1.6 %shard_map.70 = (f32[2,128,256]{2,1,0:T(8,128)}, f32[2,256,256]{2,1,0:T(8,128)}) custom-call(s32[2,4]{1,0:T(2,128)S(1)} %copy-done.6, f32[2,128,256]{2,1,0:T(8,128)S(1)} %get-tuple-element.8.bsum, f32[4,128,128]{2,1,0:T(8,128)S(1)} %bitcast.4, f32[2,256,256]{2,1,0:T(8,128)S(1)} %copy-done.3), custom_call_target="tpu_custom_call" | custom-call | tf_op jit(solution)/shard_map/pallas_call | solution.py:460
Async XLA Ops:
  0.6 1.6 %copy-start = (f32[2,1024,256]{2,1,0:T(8,128)S(1)}, f32[2,1024,256]{2,1,0:T(8,128)}, u32[]{:S(2)}) copy-start(f32[2,1024,256]{2,1,0:T(8,128)} %param.7) | copy-start | bytes 6291460
  2.2 0.7 copy-start.4
  2.9 5.2 %copy-start.1 = (f32[2,1024,256]{2,1,0:T(8,128)S(1)}, f32[2,1024,256]{2,1,0:T(8,128)}, u32[]{:S(2)}) copy-start(f32[2,1024,256]{2,1,0:T(8,128)} %param.7) | copy-start | bytes 6291460
  2.9 5.2 %copy-start.5 = (s32[2,16]{1,0:T(2,128)S(1)}, s32[2,16]{1,0:T(2,128)}, u32[]{:S(2)}) copy-start(s32[2,16]{1,0:T(2,128)} %fb_hbm.3) | copy-start | bytes 388
  2.9 5.2 %copy-start.6 = (s32[2,4]{1,0:T(2,128)S(1)}, s32[2,4]{1,0:T(2,128)}, u32[]{:S(2)}) copy-start(s32[2,4]{1,0:T(2,128)} %bounds.1) | copy-start | bytes 100
  6.1 1.9 %copy-start.2 = (f32[2,4,256,512]{3,2,1,0:T(8,128)}, f32[2,4,256,512]{3,2,1,0:T(8,128)S(1)}, u32[]{:S(2)}) copy-start(f32[2,4,256,512]{3,2,1,0:T(8,128)S(1)} %get-tuple-element.6.tiles) | copy-start | bytes 12582916
  8.1 67.3 %copy-start.3 = (f32[2,256,256]{2,1,0:T(8,128)S(1)}, f32[2,256,256]{2,1,0:T(8,128)}, u32[]{:S(2)}) copy-start(f32[2,256,256]{2,1,0:T(8,128)} %terms.1) | copy-start | bytes 1572868

commit v2 on v1

--- a/solution.py
+++ b/solution.py
@@ -21,7 +21,7 @@
     return jnp.dot(a, b, preferred_element_type=jnp.float32)
 
 
-def fetch_kernel(dims, fb_hbm, inv, panels, tiles, wsel, fb, fb_sem, sem, wsem):
+def fetch_kernel(dims, fb_hbm, inv, tiles, fb, fb_sem, sem):
     fronts, kb, n_row, n_col, nz, nx, rg, cg, nh, hw = dims
     r = lax.axis_index("row")
     c = lax.axis_index("col")
@@ -32,16 +32,6 @@
     table.wait()
     copies = []
     for f in range(fronts):
-        at = jnp.int32(0)
-        for j in range(per_owner):
-            at = jnp.where(fb[f, r * per_owner + j] // cg == c, j, at)
-        for h in range(nh):
-            copies.append(
-                pltpu.make_async_copy(
-                    panels.at[f, at, :, pl.ds(h * hw, hw)], wsel.at[f, h], wsem.at[f, h]
-                )
-            )
-            copies[-1].start()
         cols = [jnp.int32(0)] * nc
         m = jnp.int32(0)
         rows = [jnp.int32(0)] * n_row
@@ -95,13 +85,13 @@
 
 
 CUTS = 2
-AHEAD = 4
+AHEAD = 3
 
 
 def copies_of(dims):
     fronts, kb, n_row, n_col, nz, nx, rg, cg, nh, hw = dims
     gather = 2 * CUTS * (n_row // 2 - 1) + 1
-    sums = n_row * (nx - 1) + (n_row - 1) + (nz - 1)
+    sums = n_row * (nx - 1) + (n_row - 1) + 3
     diag = 2 * (n_row * nx - 1) + (nz - 1)
     return fronts * nh * (gather + sums + diag)
 
@@ -117,8 +107,8 @@
 
 
 def main_kernel(
-    dims, fb_hbm, bounds_hbm, tiles, wsel, panels, bsum, pkall,
-    fb, bounds, th, tl, bm, wb, part, xbuf, xs, rbuf, qs, zbuf, pan, pth, ptl,
+    dims, fb_hbm, bounds_hbm, tiles, panels, bsum, pkall,
+    fb, bounds, th, tl, bm, wb, part, xbuf, xs, rbuf, qs, zbuf, zs, pth, ptl,
     dpk, rsb, zb, local_sem, send_sem, recv_sem,
 ):
     fronts, kb, n_row, n_col, nz, nx, rg, cg, nh, hw = dims
@@ -156,37 +146,27 @@
     ]
     for copy in small:
         copy.start()
-    own_rows = []
-    for f in range(fronts):
-        for j in range(nz):
-            at = len(own_rows)
-            copy = pltpu.make_async_copy(
-                panels.at[f, j, pl.ds(pl.multiple_of(s * share, share), share), :],
-                pan.at[f, j],
-                local_sem.at[2 + at],
-            )
-            copy.start()
-            own_rows.append(copy)
-
-    barrier = pltpu.get_barrier_semaphore()
-    peers = [peer for _, peer in plane] + [(r, to * nx + s) for to in depth]
-    for peer in peers:
-        pl.semaphore_signal(barrier, inc=1, device_id=peer, device_id_type=MESH)
-    pl.semaphore_wait(barrier, len(peers))
     mail = Mail(send_sem, recv_sem)
     height = BS // CUTS
     line, beside, relayed = {}, {}, {}
 
+    def w_pick(i):
+        f, h = divmod(i, nh)
+        at = jnp.int32(0)
+        for j in range(per_owner):
+            at = jnp.where(fb[f, r * per_owner + j] // cg == c, j, at)
+        wb[i][r] = panels[f, at, :, h * hw : (h + 1) * hw]
+
     def w_send(i):
-        f, h = divmod(i, nh)
         line[i] = []
         for cut in range(CUTS):
             rows = pl.ds(cut * height, height)
+            piece = wb[i].at[r, rows]
             for d in range(1, ny):
-                copy = mail.send(wsel.at[f, h, rows], wb[i].at[r, rows], (row_at(d, 0), c))
+                copy = mail.send(piece, piece, (row_at(d, 0), c))
                 line[i].append((copy, row_at(ny - d, 0), rows))
-        beside[i] = mail.send(wsel.at[f, h], wb[i].at[r], (partner, c))
-        wb[i][r] = wsel[f, h]
+        piece = wb[i].at[r]
+        beside[i] = mail.send(piece, piece, (partner, c))
 
     def w_relay(i):
         relayed[i] = []
@@ -220,7 +200,8 @@
 
     def split_panels(f):
         for j in range(nz):
-            hi, lo = split(pan[f, j].T)
+            own = panels[f, j, pl.ds(pl.multiple_of(s * share, share), share), :]
+            hi, lo = split(own.T)
             pth[f, :, j * share : (j + 1) * share] = hi
             ptl[f, :, j * share : (j + 1) * share] = lo
 
@@ -273,8 +254,17 @@
             dpk[i, e] = packed[e * rows_each : (e + 1) * rows_each]
         for at, (e, peer) in enumerate(plane):
             to_plane[i, at] = mail.send(dpk.at[i, e], rsb.at[i, at], peer)
-        for d, to in enumerate(depth, 1):
-            along_z[i, d] = mail.send(qs.at[i, to], zbuf.at[i, d - 1], (r, to * nx + s))
+        near = z + 1 - 2 * lax.rem(z, 2)
+        for at in (1, 0):
+            along_z[i, at] = mail.send(
+                qs.at[i, lax.rem(near + 2 * at, nz)], zbuf.at[i, at], (r, near * nx + s)
+            )
+
+    def z_second(i):
+        far = lax.rem(z + 2, nz)
+        along_z[i, 1].wait_recv()
+        zs[i] = qs[i, far] + zbuf[i, 1]
+        along_z[i, 2] = mail.send(zs.at[i], zbuf.at[i, 2], (r, far * nx + s))
 
     def diag_sum(i):
         total = dpk[i, mine]
@@ -299,30 +289,34 @@
 
     def finish(i):
         f, h = divmod(i, nh)
-        total = qs[i, z]
-        for d in range(1, nz):
-            along_z[i, d].wait_recv()
-            total = total + zbuf[i, d - 1]
+        along_z[i, 0].wait_recv()
+        total = qs[i, z] + zbuf[i, 0]
+        along_z[i, 2].wait_recv()
+        total = total + zbuf[i, 2]
         bsum[f, :, h * hw : (h + 1) * hw] = total
 
     def done(i):
         for at in range(len(plane)):
             back[i, at].wait_recv()
 
+    barrier = pltpu.get_barrier_semaphore()
+    peers = [peer for _, peer in plane] + [(r, to * nx + s) for to in depth]
+    for peer in peers:
+        pl.semaphore_signal(barrier, inc=1, device_id=peer, device_id_type=MESH)
+    for copy in small:
+        copy.wait()
+    for i in range(chunks):
+        w_pick(i)
+    pl.semaphore_wait(barrier, len(peers))
     w_send(0)
     w_send(1)
     split_tiles(0)
-    for copy in small:
-        copy.wait()
     w_relay(0)
     w_ready(0)
     for n in range(AHEAD):
         piece_product(n)
     w_relay(1)
-    for i in range(2, chunks):
-        w_send(i)
-    for copy in own_rows:
-        copy.wait()
+    w_send(2)
     for f in range(1, fronts):
         split_tiles(f)
     for f in range(fronts):
@@ -331,14 +325,19 @@
     tasks = {}
 
     def plan(n, task, i):
-        tasks.setdefault(min(n, total_pieces - 1), []).append((task, i))
+        tasks.setdefault(min(n, total_pieces), []).append((task, i))
 
     for i in range(chunks - 1):
         last = (i + 1) * n_row - 1
-        plan(last + 2, z_stage, i)
-        plan(last + 4, diag_sum, i)
-        plan(last + 5, finish, i)
-        plan(last + 6, diag_back, i)
+        plan(last + 1, z_stage, i)
+        plan(last + 3, diag_sum, i)
+        plan(last + 4, z_second, i)
+        plan(last + 5, diag_back, i)
+        plan(last + 7, finish, i)
+    for i in range(2, chunks):
+        if i > 2:
+            plan((i - 2) * n_row - 1, w_send, i)
+        plan((i - 2) * n_row + 2, w_relay, i)
     for n in range(total_pieces):
         piece_sum(n)
         ahead = n + AHEAD
@@ -346,16 +345,14 @@
             if ahead % n_row == 0:
                 w_ready(ahead // n_row)
             piece_product(ahead)
-        if n % 2 == 1 and 2 + n // 2 < chunks:
-            w_relay(2 + n // 2)
-        if n < total_pieces - 1:
-            for task, i in tasks.get(n, []):
-                task(i)
+        for task, i in tasks.get(n, []):
+            task(i)
     last = chunks - 1
     z_stage(last)
-    for task, i in tasks.get(total_pieces - 1, []):
+    for task, i in tasks.get(total_pieces, []):
         task(i)
     diag_sum(last)
+    z_second(last)
     diag_back(last)
     finish(last)
     for i in range(chunks):
@@ -399,25 +396,21 @@
     f32, bf16 = jnp.float32, jnp.bfloat16
     vmem = pl.BlockSpec(memory_space=pltpu.VMEM)
     smem = pl.BlockSpec(memory_space=pltpu.SMEM)
-    anywhere = pl.BlockSpec(memory_space=pl.ANY)
+    anywhere = pl.BlockSpec(memory_space=pltpu.HBM)
     blocks = panels.reshape(fronts, per_owner, BS, width)
 
-    tiles, wsel = pl.pallas_call(
+    tiles = pl.pallas_call(
         functools.partial(fetch_kernel, dims),
-        out_shape=(
-            jax.ShapeDtypeStruct((fronts, n_row, BS, nc * BS), f32),
-            jax.ShapeDtypeStruct((fronts, nh, BS, hw), f32),
-        ),
-        in_specs=[anywhere, anywhere, anywhere],
-        out_specs=(vmem, vmem),
+        out_shape=jax.ShapeDtypeStruct((fronts, n_row, BS, nc * BS), f32),
+        in_specs=[anywhere, anywhere],
+        out_specs=vmem,
         scratch_shapes=[
             pltpu.SMEM((fronts, kb), jnp.int32),
             pltpu.SemaphoreType.DMA(()),
             pltpu.SemaphoreType.DMA((fronts, n_row, nc)),
-            pltpu.SemaphoreType.DMA((fronts, nh)),
         ],
         compiler_params=pltpu.CompilerParams(vmem_limit_bytes=24 << 20),
-    )(front_blocks, inverse, blocks)
+    )(front_blocks, inverse)
 
     count = copies_of(dims)
     V = pltpu.VMEM
@@ -427,7 +420,7 @@
             jax.ShapeDtypeStruct((fronts, share, width), f32),
             jax.ShapeDtypeStruct((chunks, groups, rows_each, hw), f32),
         ),
-        in_specs=[anywhere, anywhere, vmem, vmem, anywhere],
+        in_specs=[anywhere, anywhere, vmem, vmem],
         out_specs=(vmem, vmem),
         scratch_shapes=[
             pltpu.SMEM((fronts, kb), jnp.int32),
@@ -441,21 +434,23 @@
             V((chunks, n_row, share, hw), f32),
             [V((n_row, share, hw), f32)] * chunks,
             V((chunks, nz, share, hw), f32),
-            V((chunks, nz - 1, share, hw), f32),
-            V((fronts, nz, share, width), f32),
+            V((chunks, 3, share, hw), f32),
+            V((chunks, share, hw), f32),
             V((fronts, width, nz * share), bf16),
             V((fronts, width, nz * share), bf16),
             V((chunks, groups, rows_each, hw), f32),
             V((chunks, groups - 1, rows_each, hw), f32),
             V((chunks, nz, rows_each, hw), f32),
-            pltpu.SemaphoreType.DMA((2 + fronts * nz,)),
+            pltpu.SemaphoreType.DMA((2,)),
             pltpu.SemaphoreType.DMA((count,)),
             pltpu.SemaphoreType.DMA((count,)),
         ],
         compiler_params=pltpu.CompilerParams(
-            collective_id=0, has_side_effects=True, vmem_limit_bytes=48 << 20
+            collective_id=0,
+            has_side_effects=True,
+            vmem_limit_bytes=32 << 20,
         ),
-    )(front_blocks, bounds, tiles, wsel, blocks)
+    )(front_blocks, bounds, tiles, blocks)
 
     return pl.pallas_call(
         last_kernel,

time: 77.2 us -> 64 us (0.83)
  Pallas kernels: 72.2 us -> 62.5 us
  local copies, waits for them, and re-layouts: 4.21 us -> 0.69 us
    pallas_call x1, Pallas kernels: 67.3 us -> 57.7 us  [body(): pl.pallas_call(functools.partial(main_kernel, dims), out_shape=(jax.Shape...]
    unnamed x14 -> x10, local copies, waits for them, and re-layouts: 4.21 us -> 0.69 us
where the time goes in v2:
time: 64 us; the launch traced here: 63.8 us
  Pallas kernels  62.5 us (98%)
  between operations  0.7 us (1%)
  local copies, waits for them, and re-layouts  0.69 us (1%)
    pallas_call x1, Pallas kernels, body(): pl.pallas_call(functools.partial(main_kernel, dims), out_shape=(jax.Shape...  57.7 us
    pallas_call x1, Pallas kernels, body(): pl.pallas_call(functools.partial(fetch_kernel, dims), out_shape=jax.Shape...  3.13 us
    pallas_call x1, Pallas kernels, body(): pl.pallas_call(last_kernel, out_shape=(jax.ShapeDtypeStruct((fronts, shar...  1.64 us

profile of v2, /device:TPU:0, one launch (start us, length us, event | category | flops | bytes accessed | tf_op | source)
XLA Modules:
  0.0 63.8 jit_solution(13445858657340717777)
XLA Ops:
  0.6 0.0 copy-start.2
  0.6 0.7 %copy-done.2 = s32[2,16]{1,0:T(2,128)S(1)} copy-done((s32[2,16]{1,0:T(2,128)S(1)}, s32[2,16]{1,0:T(2,128)}, u32[]{:S(2)}) %copy-start.2) | copy-done | bytes 152
  1.3 0.0 copy-start
  1.3 0.0 copy-start.3
  1.3 0.0 copy-start.4
  1.3 3.1 %shard_map.68.tiles = f32[2,4,256,512]{3,2,1,0:T(8,128)S(1)} custom-call(s32[2,16]{1,0:T(2,128)S(1)} %copy-done.2, f32[4096,2048]{1,0:T(8,128)} %inv.1), custom_call_target="tpu_custom_call" | custom-call | tf_op jit(solution)/shard_map/pallas_call | solution.py:402
  4.5 0.0 copy-done
  4.5 0.0 copy-done.3
  4.5 0.0 copy-done.4
  4.5 0.0 copy-start.1
  4.5 57.7 %shard_map.69 = (f32[2,128,256]{2,1,0:T(8,128)S(1)}, f32[4,8,16,128]{3,2,1,0:T(8,128)S(1)}) custom-call(s32[2,16]{1,0:T(2,128)S(1)} %copy-done.3, s32[2,4]{1,0:T(2,128)S(1)} %copy-done.4, f32[2,4,256,512]{3,2,1,0:T(8,128)S(1)} %shard_map.68.tiles, f32[2,4,256,256]{3,2,1,0:T(8,128)S(1)} %bitcast.2), custom_call_target="tpu_custom_call" | custom-call | tf_op jit(solution)/shard_map/pallas_call | solution.py:417
  62.2 0.0 copy-done.1
  62.2 1.6 %shard_map.70 = (f32[2,128,256]{2,1,0:T(8,128)}, f32[2,256,256]{2,1,0:T(8,128)}) custom-call(s32[2,4]{1,0:T(2,128)S(1)} %copy-done.4, f32[2,128,256]{2,1,0:T(8,128)S(1)} %get-tuple-element.4.bsum, f32[4,128,128]{2,1,0:T(8,128)S(1)} %bitcast.3, f32[2,256,256]{2,1,0:T(8,128)S(1)} %copy-done.1), custom_call_target="tpu_custom_call" | custom-call | tf_op jit(solution)/shard_map/pallas_call | solution.py:455
Async XLA Ops:
  0.6 0.7 %copy-start.2 = (s32[2,16]{1,0:T(2,128)S(1)}, s32[2,16]{1,0:T(2,128)}, u32[]{:S(2)}) copy-start(s32[2,16]{1,0:T(2,128)} %fb_hbm.3) | copy-start | bytes 388
  1.3 3.1 %copy-start = (f32[2,1024,256]{2,1,0:T(8,128)S(1)}, f32[2,1024,256]{2,1,0:T(8,128)}, u32[]{:S(2)}) copy-start(f32[2,1024,256]{2,1,0:T(8,128)} %param.7) | copy-start | bytes 6291460
  1.3 3.2 %copy-start.3 = (s32[2,16]{1,0:T(2,128)S(1)}, s32[2,16]{1,0:T(2,128)}, u32[]{:S(2)}) copy-start(s32[2,16]{1,0:T(2,128)} %fb_hbm.3) | copy-start | bytes 388
  1.3 3.2 %copy-start.4 = (s32[2,4]{1,0:T(2,128)S(1)}, s32[2,4]{1,0:T(2,128)}, u32[]{:S(2)}) copy-start(s32[2,4]{1,0:T(2,128)} %bounds.1) | copy-start | bytes 100
  4.5 57.7 %copy-start.1 = (f32[2,256,256]{2,1,0:T(8,128)S(1)}, f32[2,256,256]{2,1,0:T(8,128)}, u32[]{:S(2)}) copy-start(f32[2,256,256]{2,1,0:T(8,128)} %terms.1) | copy-start | bytes 1572868

commit v3 on v2

--- a/solution.py
+++ b/solution.py
@@ -85,7 +85,7 @@
 
 
 CUTS = 2
-AHEAD = 3
+AHEAD = 4
 
 
 def copies_of(dims):
@@ -109,7 +109,7 @@
 def main_kernel(
     dims, fb_hbm, bounds_hbm, tiles, panels, bsum, pkall,
     fb, bounds, th, tl, bm, wb, part, xbuf, xs, rbuf, qs, zbuf, zs, pth, ptl,
-    dpk, rsb, zb, local_sem, send_sem, recv_sem,
+    dpk, csb, hs, rsb, zb, local_sem, send_sem, recv_sem,
 ):
     fronts, kb, n_row, n_col, nz, nx, rg, cg, nh, hw = dims
     r = lax.axis_index("row")
@@ -131,13 +131,20 @@
     offsets = [(dy, dk) for dy in range(1, ny) for dk in range(2)] + [(0, 1), (0, 0)]
     slots = [row_at(dy, dk) for dy, dk in offsets]
     partner = row_at(0, 1)
-    mine = r * nx + s
-    plane = []
+    half_groups = ny * nx
+    other = 1 - core
+    flat_mine = y * nx + s
+    mine = core * half_groups + flat_mine
+    plane, flat = [], []
     for dy, dk in offsets:
         for ds in range(nx):
             if (dy, dk, ds) != (0, 0, 0):
                 row, x = row_at(dy, dk), lax.rem(s + ds, nx)
-                plane.append((row * nx + x, (row, z * nx + x)))
+                e = lax.rem(y + dy, ny) * nx + x
+                peer = (row, z * nx + x)
+                plane.append((lax.rem(core + dk, 2) * half_groups + e, peer))
+                if dk == 0:
+                    flat.append((e, peer))
     depth = [lax.rem(z + d, nz) for d in range(1, nz)]
 
     small = [
@@ -235,9 +242,9 @@
             xs[i, o] = total
             along_row[i, o] = mail.send(xs.at[i, o], rbuf[i].at[r], (slots[o], c))
 
-    to_plane, to_depth, back = {}, {}, {}
-
-    def z_stage(i):
+    to_core, to_plane, to_depth, back, to_half = {}, {}, {}, {}, {}
+
+    def z_diag(i):
         f, h = divmod(i, nh)
         for o in range(n_row - 1):
             along_row[i, o].wait_recv()
@@ -252,10 +259,17 @@
         packed = jnp.where(same, inner[:half], inner[half:])
         for e in range(groups):
             dpk[i, e] = packed[e * rows_each : (e + 1) * rows_each]
-        for at, (e, peer) in enumerate(plane):
-            to_plane[i, at] = mail.send(dpk.at[i, e], rsb.at[i, at], peer)
+        if i == chunks - 1:
+            for at, (e, peer) in enumerate(plane):
+                to_plane[i, at] = mail.send(dpk.at[i, e], rsb.at[i, at], peer)
+        else:
+            to_core[i] = mail.send(
+                dpk.at[i, pl.ds(other * half_groups, half_groups)], csb.at[i], (partner, c)
+            )
+
+    def z_first(i, slots_sent=(1, 0)):
         near = z + 1 - 2 * lax.rem(z, 2)
-        for at in (1, 0):
+        for at in slots_sent:
             along_z[i, at] = mail.send(
                 qs.at[i, lax.rem(near + 2 * at, nz)], zbuf.at[i, at], (r, near * nx + s)
             )
@@ -266,9 +280,18 @@
         zs[i] = qs[i, far] + zbuf[i, 1]
         along_z[i, 2] = mail.send(zs.at[i], zbuf.at[i, 2], (r, far * nx + s))
 
+    def diag_half(i):
+        to_core[i].wait_recv()
+        hs[i] = dpk[i, pl.ds(core * half_groups, half_groups)] + csb[i]
+        for at, (e, peer) in enumerate(flat):
+            to_plane[i, at] = mail.send(hs.at[i, e], rsb.at[i, at], peer)
+
     def diag_sum(i):
-        total = dpk[i, mine]
-        for at in range(len(plane)):
+        if i == chunks - 1:
+            total, count = dpk[i, mine], len(plane)
+        else:
+            total, count = hs[i, flat_mine], len(flat)
+        for at in range(count):
             to_plane[i, at].wait_recv()
             total = total + rsb[i, at]
         zb[i, z] = total
@@ -283,9 +306,15 @@
         for j in range(1, nz):
             total = total + zb[i, j]
         pkall[i, mine] = total
-        for at, (_, peer) in enumerate(plane):
+        for at, (_, peer) in enumerate(plane if i == chunks - 1 else flat):
             piece = pkall.at[i, mine]
             back[i, at] = mail.send(piece, piece, peer)
+
+    def diag_share(i):
+        for at in range(len(flat)):
+            back[i, at].wait_recv()
+        piece = pkall.at[i, pl.ds(core * half_groups, half_groups)]
+        to_half[i] = mail.send(piece, piece, (partner, c))
 
     def finish(i):
         f, h = divmod(i, nh)
@@ -296,8 +325,11 @@
         bsum[f, :, h * hw : (h + 1) * hw] = total
 
     def done(i):
-        for at in range(len(plane)):
-            back[i, at].wait_recv()
+        if i == chunks - 1:
+            for at in range(len(plane)):
+                back[i, at].wait_recv()
+        else:
+            to_half[i].wait_recv()
 
     barrier = pltpu.get_barrier_semaphore()
     peers = [peer for _, peer in plane] + [(r, to * nx + s) for to in depth]
@@ -309,37 +341,41 @@
         w_pick(i)
     pl.semaphore_wait(barrier, len(peers))
     w_send(0)
+    for f in range(fronts):
+        split_tiles(f)
+    for f in range(fronts):
+        split_panels(f)
     w_send(1)
-    split_tiles(0)
     w_relay(0)
     w_ready(0)
     for n in range(AHEAD):
         piece_product(n)
+    w_send(2)
     w_relay(1)
-    w_send(2)
-    for f in range(1, fronts):
-        split_tiles(f)
-    for f in range(fronts):
-        split_panels(f)
 
     tasks = {}
 
     def plan(n, task, i):
-        tasks.setdefault(min(n, total_pieces), []).append((task, i))
-
-    for i in range(chunks - 1):
-        last = (i + 1) * n_row - 1
-        plan(last + 1, z_stage, i)
-        plan(last + 3, diag_sum, i)
-        plan(last + 4, z_second, i)
-        plan(last + 5, diag_back, i)
-        plan(last + 7, finish, i)
+        if i < chunks - 1 or task in (w_send, w_relay):
+            tasks.setdefault(min(n, total_pieces), []).append((task, i))
+
     for i in range(2, chunks):
         if i > 2:
             plan((i - 2) * n_row - 1, w_send, i)
         plan((i - 2) * n_row + 2, w_relay, i)
+    for i in range(chunks):
+        last = (i + 1) * n_row - 1
+        plan(last + 2, diag_half, i)
+        plan(last + 4, z_second, i)
+        plan(last + 7, diag_sum, i)
+        plan(last + 9, finish, i)
+        plan(last + 11, diag_back, i)
+        plan(last + 14, diag_share, i)
     for n in range(total_pieces):
         piece_sum(n)
+        if n >= n_row and n % n_row == 0:
+            z_diag(n // n_row - 1)
+            z_first(n // n_row - 1)
         ahead = n + AHEAD
         if ahead < total_pieces:
             if ahead % n_row == 0:
@@ -348,12 +384,29 @@
         for task, i in tasks.get(n, []):
             task(i)
     last = chunks - 1
-    z_stage(last)
-    for task, i in tasks.get(total_pieces, []):
-        task(i)
+    late = tasks.get(total_pieces, [])
+
+    def run(i, *wanted):
+        for task, at in late:
+            if at == i and task in wanted:
+                task(at)
+
+    for i in range(last - 1):
+        run(i, z_second, diag_half, diag_sum)
+    run(last - 1, z_second, diag_half)
+    z_diag(last)
+    z_first(last, (1,))
+    for i in range(last - 1):
+        run(i, finish, diag_back)
+    run(last - 1, diag_sum)
+    z_first(last, (0,))
     diag_sum(last)
     z_second(last)
+    run(last - 1, diag_back)
+    for i in range(last - 1):
+        run(i, diag_share)
     diag_back(last)
+    run(last - 1, finish, diag_share)
     finish(last)
     for i in range(chunks):
         done(i)
@@ -439,6 +492,8 @@
             V((fronts, width, nz * share), bf16),
             V((fronts, width, nz * share), bf16),
             V((chunks, groups, rows_each, hw), f32),
+            V((chunks, groups // 2, rows_each, hw), f32),
+            V((chunks, groups // 2, rows_each, hw), f32),
             V((chunks, groups - 1, rows_each, hw), f32),
             V((chunks, nz, rows_each, hw), f32),
             pltpu.SemaphoreType.DMA((2,)),

time: 64 us -> 57.3 us (0.90)
  Pallas kernels: 62.5 us -> 55.8 us
    pallas_call x1, Pallas kernels: 57.7 us -> 51 us  [body(): pl.pallas_call(functools.partial(main_kernel, dims), out_shape=(jax.Shape...]
where the time goes in v3:
time: 57.3 us; the launch traced here: 57.2 us
  Pallas kernels  55.8 us (97%)
  between operations  0.7 us (1%)
  local copies, waits for them, and re-layouts  0.69 us (1%)
    pallas_call x1, Pallas kernels, body(): pl.pallas_call(functools.partial(main_kernel, dims), out_shape=(jax.Shape...  51 us
    pallas_call x1, Pallas kernels, body(): pl.pallas_call(functools.partial(fetch_kernel, dims), out_shape=jax.Shape...  3.13 us
    pallas_call x1, Pallas kernels, body(): pl.pallas_call(last_kernel, out_shape=(jax.ShapeDtypeStruct((fronts, shar...  1.64 us

profile of v3, /device:TPU:0, one launch (start us, length us, event | category | flops | bytes accessed | tf_op | source)
XLA Modules:
  0.0 57.2 jit_solution(1180491047687071190)
XLA Ops:
  0.6 0.0 copy-start.2
  0.6 0.7 %copy-done.2 = s32[2,16]{1,0:T(2,128)S(1)} copy-done((s32[2,16]{1,0:T(2,128)S(1)}, s32[2,16]{1,0:T(2,128)}, u32[]{:S(2)}) %copy-start.2) | copy-done | bytes 152
  1.3 0.0 copy-start
  1.3 0.0 copy-start.3
  1.3 0.0 copy-start.4
  1.3 3.1 %shard_map.68.tiles = f32[2,4,256,512]{3,2,1,0:T(8,128)S(1)} custom-call(s32[2,16]{1,0:T(2,128)S(1)} %copy-done.2, f32[4096,2048]{1,0:T(8,128)} %inv.1), custom_call_target="tpu_custom_call" | custom-call | tf_op jit(solution)/shard_map/pallas_call | solution.py:455
  4.5 0.0 copy-done
  4.5 0.0 copy-done.3
  4.5 0.0 copy-done.4
  4.5 0.0 copy-start.1
  4.5 51.0 %shard_map.69 = (f32[2,128,256]{2,1,0:T(8,128)S(1)}, f32[4,8,16,128]{3,2,1,0:T(8,128)S(1)}) custom-call(s32[2,16]{1,0:T(2,128)S(1)} %copy-done.3, s32[2,4]{1,0:T(2,128)S(1)} %copy-done.4, f32[2,4,256,512]{3,2,1,0:T(8,128)S(1)} %shard_map.68.tiles, f32[2,4,256,256]{3,2,1,0:T(8,128)S(1)} %bitcast.2), custom_call_target="tpu_custom_call" | custom-call | tf_op jit(solution)/shard_map/pallas_call | solution.py:470
  55.5 0.0 copy-done.1
  55.5 1.6 %shard_map.70 = (f32[2,128,256]{2,1,0:T(8,128)}, f32[2,256,256]{2,1,0:T(8,128)}) custom-call(s32[2,4]{1,0:T(2,128)S(1)} %copy-done.4, f32[2,128,256]{2,1,0:T(8,128)S(1)} %get-tuple-element.4.bsum, f32[4,128,128]{2,1,0:T(8,128)S(1)} %bitcast.3, f32[2,256,256]{2,1,0:T(8,128)S(1)} %copy-done.1), custom_call_target="tpu_custom_call" | custom-call | tf_op jit(solution)/shard_map/pallas_call | solution.py:510
Async XLA Ops:
  0.6 0.7 %copy-start.2 = (s32[2,16]{1,0:T(2,128)S(1)}, s32[2,16]{1,0:T(2,128)}, u32[]{:S(2)}) copy-start(s32[2,16]{1,0:T(2,128)} %fb_hbm.3) | copy-start | bytes 388
  1.3 3.1 %copy-start = (f32[2,1024,256]{2,1,0:T(8,128)S(1)}, f32[2,1024,256]{2,1,0:T(8,128)}, u32[]{:S(2)}) copy-start(f32[2,1024,256]{2,1,0:T(8,128)} %param.7) | copy-start | bytes 6291460
  1.3 3.2 %copy-start.3 = (s32[2,16]{1,0:T(2,128)S(1)}, s32[2,16]{1,0:T(2,128)}, u32[]{:S(2)}) copy-start(s32[2,16]{1,0:T(2,128)} %fb_hbm.3) | copy-start | bytes 388
  1.3 3.2 %copy-start.4 = (s32[2,4]{1,0:T(2,128)S(1)}, s32[2,4]{1,0:T(2,128)}, u32[]{:S(2)}) copy-start(s32[2,4]{1,0:T(2,128)} %bounds.1) | copy-start | bytes 100
  4.5 51.0 %copy-start.1 = (f32[2,256,256]{2,1,0:T(8,128)S(1)}, f32[2,256,256]{2,1,0:T(8,128)}, u32[]{:S(2)}) copy-start(f32[2,256,256]{2,1,0:T(8,128)} %terms.1) | copy-start | bytes 1572868

commit v4 on v3

--- a/solution.py
+++ b/solution.py
@@ -93,7 +93,8 @@
     gather = 2 * CUTS * (n_row // 2 - 1) + 1
     sums = n_row * (nx - 1) + (n_row - 1) + 3
     diag = 2 * (n_row * nx - 1) + (nz - 1)
-    return fronts * nh * (gather + sums + diag)
+    first = 3 + (nx - 1) + (n_row - 1) + (nz - 1)
+    return fronts * nh * (gather + sums + diag) + first
 
 
 def node_ids(bounds, f, first, shape, dim):
@@ -109,6 +110,7 @@
 def main_kernel(
     dims, fb_hbm, bounds_hbm, tiles, panels, bsum, pkall,
     fb, bounds, th, tl, bm, wb, part, xbuf, xs, rbuf, qs, zbuf, zs, pth, ptl,
+    pfh, pfl, own_u, par_s, par_r, p0, zn, fs, zf, x0, x0r, rs0, rb0, q0, zc, inner0, tah, tal, tbh, tbl,
     dpk, csb, hs, rsb, zb, local_sem, send_sem, recv_sem,
 ):
     fronts, kb, n_row, n_col, nz, nx, rg, cg, nh, hw = dims
@@ -119,11 +121,22 @@
     per_owner = kb // n_row
     nc = kb // n_col
     share = BS // nx
+    width = panels.shape[3]
     chunks = fronts * nh
+    if chunks != 4 or nz != 4:
+        raise ValueError(chunks, nz)
     groups = n_row * nx
     half = dpk.shape[1] * dpk.shape[2]
     rows_each = dpk.shape[2]
+    last = chunks - 1
+    direct = (0, last - 1, last)
+    wide = (last,)
     total_pieces = chunks * n_row
+    near = z + 1 - 2 * lax.rem(z, 2)
+    far = lax.rem(z + 2, nz)
+    sh2 = share // 2
+    e0 = sh2 // nz
+    kept = [sh2] + [share] * last
 
     def row_at(dy, dk):
         return lax.rem(y + dy, ny) * 2 + lax.rem(core + dk, 2)
@@ -209,57 +222,139 @@
         for j in range(nz):
             own = panels[f, j, pl.ds(pl.multiple_of(s * share, share), share), :]
             hi, lo = split(own.T)
-            pth[f, :, j * share : (j + 1) * share] = hi
-            ptl[f, :, j * share : (j + 1) * share] = lo
+            pth[f, j] = hi
+            ptl[f, j] = lo
+            hi, lo = split(panels[f, j].T)
+            pfh[f, j] = hi
+            pfl[f, j] = lo
+
+    def split_first():
+        upper = pl.ds(pl.multiple_of(s * share, share), sh2)
+        lower = pl.ds(pl.multiple_of(s * share + sh2 + z * e0, e0), e0)
+        for j in range(nz):
+            hi, lo = split(panels[0, j, upper, :].T)
+            tah[:, j * sh2 : (j + 1) * sh2] = hi
+            tal[:, j * sh2 : (j + 1) * sh2] = lo
+        own = jnp.concatenate([panels[0, j, lower, :] for j in range(nz)], axis=0)
+        hi, lo = split(own.T)
+        tbh[...] = hi
+        tbl[...] = lo
 
     along_x, along_row, along_z = {}, {}, {}
-
-    def piece_product(n):
-        i, o = divmod(n, n_row)
-        f = i // nh
-        t = slots[o]
-        both = dot(th[f, t], bm[i])
-        low = dot(tl[f, t], bm[i, :, :hw])
-        total = both[:, :hw] + (both[:, hw:] + low)
-        for to in range(nx):
-            part[i, o, to] = total[to * share : (to + 1) * share]
+    to_core, to_plane, to_depth, back, to_half = {}, {}, {}, {}, {}
+
+    def x_peers():
         for d in range(1, nx):
             to = lax.rem(s + d, nx)
+            yield d, to, (r, z * nx + to)
+
+    order = [divmod(n, n_row) for n in range(total_pieces)]
+    order.remove((last - 1, n_row - 1))
+    order.insert(order.index((last, n_row - 2)), (last - 1, n_row - 1))
+
+    def piece_product(n):
+        i, o = order[n]
+        f, keep = i // nh, kept[i]
+        both = dot(th[f, slots[o]], bm[i])
+        low = dot(tl[f, slots[o]], bm[i, :, :hw])
+        total = both[:, :hw] + (both[:, hw:] + low)
+        if i > 0 and o == n_row - 1:
+            own_u[i] = total
+        if i > 0 and o == n_row - 2:
+            par_s[i] = total
+            along_row[i, "whole"] = mail.send(par_s.at[i], par_r.at[i], (partner, c))
+        for to in range(nx):
+            part[i, o, to, :keep] = total[to * share : to * share + keep]
+        rows = pl.ds(0, keep)
+        for d, to, peer in x_peers():
             along_x[n, d] = mail.send(
-                part.at[i, o, to], xbuf.at[i, o, d - 1], (r, z * nx + to)
+                part.at[i, o, to, rows], xbuf.at[i, o, d - 1, rows], peer
             )
+        if i > 0:
+            return
+        for x in range(nx):
+            for q in range(nz):
+                at = x * share + sh2 + q * e0
+                p0[q, o, x] = total[at : at + e0]
+        if o == n_row - 1:
+            for at in (1, 0):
+                along_z["near", at] = mail.send(
+                    p0.at[lax.rem(near + 2 * at, nz)], zn.at[at], (r, near * nx + s)
+                )
 
     def piece_sum(n):
-        i, o = divmod(n, n_row)
+        i, o = order[n]
+        keep = kept[i]
+        total = part[i, o, s, :keep]
         for d in range(1, nx):
             along_x[n, d].wait_recv()
-        total = part[i, o, s]
+            total = total + xbuf[i, o, d - 1, :keep]
+        if o == n_row - 1:
+            rbuf[i][r, :keep] = total
+        else:
+            xs[i, o, :keep] = total
+            rows = pl.ds(0, keep)
+            along_row[i, o] = mail.send(
+                xs.at[i, o, rows], rbuf[i].at[r, rows], (slots[o], c)
+            )
+
+    def first_far():
+        along_z["near", 1].wait_recv()
+        fs[...] = p0[far] + zn[1]
+        along_z["far"] = mail.send(fs, zf, (r, far * nx + s))
+
+    def first_x():
+        along_z["near", 0].wait_recv()
+        along_z["far"].wait_recv()
+        for x in range(nx):
+            for o in range(n_row):
+                x0[x, o] = p0[z, o, x] + zn[0, o, x] + zf[o, x]
+        for d, to, peer in x_peers():
+            along_x["first", d] = mail.send(x0.at[to], x0r.at[d - 1], peer)
+
+    def first_row():
         for d in range(1, nx):
-            total = total + xbuf[i, o, d - 1]
-        if o == n_row - 1:
-            rbuf[i][r] = total
-        else:
-            xs[i, o] = total
-            along_row[i, o] = mail.send(xs.at[i, o], rbuf[i].at[r], (slots[o], c))
-
-    to_core, to_plane, to_depth, back, to_half = {}, {}, {}, {}, {}
-
-    def z_diag(i):
+            along_x["first", d].wait_recv()
+        for o in range(n_row):
+            total = x0[s, o]
+            for d in range(1, nx):
+                total = total + x0r[d - 1, o]
+            if o == n_row - 1:
+                rb0[r] = total
+            else:
+                rs0[o] = total
+                along_row["first", o] = mail.send(rs0.at[o], rb0.at[r], (slots[o], c))
+
+    def first_join():
+        for o in range(n_row - 1):
+            along_row["first", o].wait_recv()
+        for j in range(nz):
+            q0[j] = rb0[fb[0, r * per_owner + j] // rg]
+        whole = jnp.concatenate([q0[j] for j in range(nz)], axis=0)
+        diag_start(0, inner_product(whole, tbh, tbl) + inner0[...])
+        zc[z] = q0[z]
+        for d, to in enumerate(depth, 1):
+            along_z["owner", d] = mail.send(q0.at[to], zc.at[z], (r, to * nx + s))
+
+    def first_finish():
+        for d in range(1, nz):
+            along_z["owner", d].wait_recv()
+        for q in range(nz):
+            bsum[0, sh2 + q * e0 : sh2 + (q + 1) * e0, :hw] = zc[q]
+
+    def inner_product(whole, left_hi, left_lo):
+        hi, lo = split(whole)
+        both = dot(left_hi[...], jnp.concatenate([hi, lo], axis=1))
+        return both[:, :hw] + (both[:, hw:] + dot(left_lo[...], hi))
+
+    def diag_start(i, inner):
         f, h = divmod(i, nh)
-        for o in range(n_row - 1):
-            along_row[i, o].wait_recv()
-        for j in range(nz):
-            qs[i, j] = rbuf[i][fb[f, r * per_owner + j] // rg]
-        whole = jnp.concatenate([qs[i, j] for j in range(nz)], axis=0)
-        hi, lo = split(whole)
-        both = dot(pth[f], jnp.concatenate([hi, lo], axis=1))
-        inner = both[:, :hw] + (both[:, hw:] + dot(ptl[f], hi))
         ids = node_ids(bounds, f, 0, (half, hw), 0)
         same = ids == node_ids(bounds, f, h * hw, (half, hw), 1)
         packed = jnp.where(same, inner[:half], inner[half:])
         for e in range(groups):
             dpk[i, e] = packed[e * rows_each : (e + 1) * rows_each]
-        if i == chunks - 1:
+        if i in direct:
             for at, (e, peer) in enumerate(plane):
                 to_plane[i, at] = mail.send(dpk.at[i, e], rsb.at[i, at], peer)
         else:
@@ -267,18 +362,63 @@
                 dpk.at[i, pl.ds(other * half_groups, half_groups)], csb.at[i], (partner, c)
             )
 
+    arrived = set()
+
+    def row_wait(i, o):
+        if (i, o) not in arrived:
+            arrived.add((i, o))
+            along_row[i, o].wait_recv()
+
+    def position(f, g):
+        at = jnp.int32(0)
+        found = jnp.int32(0)
+        for j in range(nz):
+            hit = fb[f, r * per_owner + j] // rg == g
+            at = jnp.where(hit, j, at)
+            found = jnp.where(hit, 1, found)
+        return at, found
+
+    def diag_go(i):
+        f = i // nh
+        inner = jnp.zeros((width, hw), jnp.float32)
+        along_row[i, "whole"].wait_recv()
+        sources = [(r, own_u[i], pfh, pfl), (partner, par_r[i], pfh, pfl)]
+        for o in range(n_row - 2):
+            row_wait(i, o)
+        for o in range(n_row - 2):
+            sources.append((slots[o], rbuf[i][slots[o]], pth, ptl))
+        for g, block, left_hi, left_lo in sources:
+            j, found = position(f, g)
+            if n_row != nz:
+                block = jnp.where(found == 1, block, 0.0)
+            inner = inner + inner_product(block, left_hi.at[f, j], left_lo.at[f, j])
+        diag_start(i, inner)
+
+    def z_diag(i):
+        f, keep = i // nh, kept[i]
+        for o in range(n_row - 1):
+            row_wait(i, o)
+        for j in range(nz):
+            qs[i, j, :keep] = rbuf[i][fb[f, r * per_owner + j] // rg, :keep]
+        if i == 0:
+            whole = jnp.concatenate([qs[i, j, :keep] for j in range(nz)], axis=0)
+            inner0[...] = inner_product(whole, tah, tal)
+
     def z_first(i, slots_sent=(1, 0)):
-        near = z + 1 - 2 * lax.rem(z, 2)
+        rows = pl.ds(0, kept[i])
         for at in slots_sent:
             along_z[i, at] = mail.send(
-                qs.at[i, lax.rem(near + 2 * at, nz)], zbuf.at[i, at], (r, near * nx + s)
+                qs.at[i, lax.rem(near + 2 * at, nz), rows],
+                zbuf.at[i, at, rows],
+                (r, near * nx + s),
             )
 
     def z_second(i):
-        far = lax.rem(z + 2, nz)
+        keep = kept[i]
         along_z[i, 1].wait_recv()
-        zs[i] = qs[i, far] + zbuf[i, 1]
-        along_z[i, 2] = mail.send(zs.at[i], zbuf.at[i, 2], (r, far * nx + s))
+        zs[i, :keep] = qs[i, far, :keep] + zbuf[i, 1, :keep]
+        rows = pl.ds(0, keep)
+        along_z[i, 2] = mail.send(zs.at[i, rows], zbuf.at[i, 2, rows], (r, far * nx + s))
 
     def diag_half(i):
         to_core[i].wait_recv()
@@ -287,7 +427,7 @@
             to_plane[i, at] = mail.send(hs.at[i, e], rsb.at[i, at], peer)
 
     def diag_sum(i):
-        if i == chunks - 1:
+        if i in direct:
             total, count = dpk[i, mine], len(plane)
         else:
             total, count = hs[i, flat_mine], len(flat)
@@ -306,7 +446,7 @@
         for j in range(1, nz):
             total = total + zb[i, j]
         pkall[i, mine] = total
-        for at, (_, peer) in enumerate(plane if i == chunks - 1 else flat):
+        for at, (_, peer) in enumerate(plane if i in wide else flat):
             piece = pkall.at[i, mine]
             back[i, at] = mail.send(piece, piece, peer)
 
@@ -318,14 +458,14 @@
 
     def finish(i):
         f, h = divmod(i, nh)
+        keep = kept[i]
         along_z[i, 0].wait_recv()
-        total = qs[i, z] + zbuf[i, 0]
+        total = qs[i, z, :keep] + zbuf[i, 0, :keep]
         along_z[i, 2].wait_recv()
-        total = total + zbuf[i, 2]
-        bsum[f, :, h * hw : (h + 1) * hw] = total
+        bsum[f, :keep, h * hw : (h + 1) * hw] = total + zbuf[i, 2, :keep]
 
     def done(i):
-        if i == chunks - 1:
+        if i in wide:
             for at in range(len(plane)):
                 back[i, at].wait_recv()
         else:
@@ -350,63 +490,69 @@
     w_ready(0)
     for n in range(AHEAD):
         piece_product(n)
+    w_relay(1)
     w_send(2)
-    w_relay(1)
+    split_first()
 
     tasks = {}
 
-    def plan(n, task, i):
-        if i < chunks - 1 or task in (w_send, w_relay):
-            tasks.setdefault(min(n, total_pieces), []).append((task, i))
-
-    for i in range(2, chunks):
-        if i > 2:
-            plan((i - 2) * n_row - 1, w_send, i)
-        plan((i - 2) * n_row + 2, w_relay, i)
-    for i in range(chunks):
-        last = (i + 1) * n_row - 1
-        plan(last + 2, diag_half, i)
-        plan(last + 4, z_second, i)
-        plan(last + 7, diag_sum, i)
-        plan(last + 9, finish, i)
-        plan(last + 11, diag_back, i)
-        plan(last + 14, diag_share, i)
+    def plan(n, task, *args):
+        tasks.setdefault(n, []).append((task, args))
+
+    plan(n_row - 1, first_far)
+    plan(n_row - 1, w_send, last)
+    for i in range(last):
+        end = order.index((i, n_row - 1))
+        at = end + 1 if i == 0 else end
+        plan(at, z_diag, i)
+        plan(at, z_first, i)
+        if end + 3 < total_pieces:
+            plan(end + 3 + (i == 0), z_second, i)
+    plan(2 * n_row - 1, diag_go, 1)
+    plan(2 * n_row + 1, diag_half, 1)
+    plan(max(3 * n_row - 1, order.index((2, n_row - 1)) - AHEAD), diag_go, 2)
+    if 2 not in direct:
+        plan(3 * n_row + 1, diag_half, 2)
+    plan(total_pieces - 2, diag_go, last)
+    plan(total_pieces - 3, diag_sum, 1)
+    plan(3 * n_row - 2, finish, 0)
+    plan(3 * n_row - 2, first_row)
+    plan(total_pieces - 3, first_join)
     for n in range(total_pieces):
         piece_sum(n)
-        if n >= n_row and n % n_row == 0:
-            z_diag(n // n_row - 1)
-            z_first(n // n_row - 1)
+        if n == 2 * n_row - 2:
+            first_x()
         ahead = n + AHEAD
         if ahead < total_pieces:
-            if ahead % n_row == 0:
-                w_ready(ahead // n_row)
+            i = order[ahead][0]
+            if i > 0 and order[ahead][1] == 0:
+                if i == 2:
+                    w_relay(2)
+                if i == last:
+                    w_relay(last)
+                w_ready(i)
             piece_product(ahead)
-        for task, i in tasks.get(n, []):
-            task(i)
-    last = chunks - 1
-    late = tasks.get(total_pieces, [])
-
-    def run(i, *wanted):
-        for task, at in late:
-            if at == i and task in wanted:
-                task(at)
-
-    for i in range(last - 1):
-        run(i, z_second, diag_half, diag_sum)
-    run(last - 1, z_second, diag_half)
+        for task, args in tasks.get(n, []):
+            task(*args)
     z_diag(last)
+    if order.index((2, n_row - 1)) + 3 >= total_pieces:
+        z_second(last - 1)
+    diag_sum(2)
+    diag_sum(0)
     z_first(last, (1,))
-    for i in range(last - 1):
-        run(i, finish, diag_back)
-    run(last - 1, diag_sum)
+    diag_sum(last)
+    diag_back(1)
+    z_second(last)
     z_first(last, (0,))
-    diag_sum(last)
-    z_second(last)
-    run(last - 1, diag_back)
-    for i in range(last - 1):
-        run(i, diag_share)
+    diag_back(2)
+    diag_back(0)
+    diag_share(1)
     diag_back(last)
-    run(last - 1, finish, diag_share)
+    diag_share(2)
+    diag_share(0)
+    finish(1)
+    finish(2)
+    first_finish()
     finish(last)
     for i in range(chunks):
         done(i)
@@ -445,6 +591,8 @@
     chunks = fronts * nh
     groups = n_row * nx
     rows_each = half // groups
+    sh2 = share // 2
+    e0 = sh2 // nz
     dims = (fronts, kb, n_row, n_col, nz, nx, rg, cg, nh, hw)
     f32, bf16 = jnp.float32, jnp.bfloat16
     vmem = pl.BlockSpec(memory_space=pltpu.VMEM)
@@ -489,8 +637,28 @@
             V((chunks, nz, share, hw), f32),
             V((chunks, 3, share, hw), f32),
             V((chunks, share, hw), f32),
-            V((fronts, width, nz * share), bf16),
-            V((fronts, width, nz * share), bf16),
+            V((fronts, nz, width, share), bf16),
+            V((fronts, nz, width, share), bf16),
+            V((fronts, nz, width, BS), bf16),
+            V((fronts, nz, width, BS), bf16),
+            V((chunks, BS, hw), f32),
+            V((chunks, BS, hw), f32),
+            V((chunks, BS, hw), f32),
+            V((nz, n_row, nx, e0, hw), f32),
+            V((2, n_row, nx, e0, hw), f32),
+            V((n_row, nx, e0, hw), f32),
+            V((n_row, nx, e0, hw), f32),
+            V((nx, n_row, e0, hw), f32),
+            V((nx - 1, n_row, e0, hw), f32),
+            V((n_row, e0, hw), f32),
+            V((n_row, e0, hw), f32),
+            V((nz, e0, hw), f32),
+            V((nz, e0, hw), f32),
+            V((width, hw), f32),
+            V((width, nz * sh2), bf16),
+            V((width, nz * sh2), bf16),
+            V((width, nz * e0), bf16),
+            V((width, nz * e0), bf16),
             V((chunks, groups, rows_each, hw), f32),
             V((chunks, groups // 2, rows_each, hw), f32),
             V((chunks, groups // 2, rows_each, hw), f32),

time: 57.3 us -> 55.9 us (0.976)
  Pallas kernels: 55.8 us -> 54.4 us
    pallas_call x1, Pallas kernels: 51 us -> 49.6 us  [body(): pl.pallas_call(functools.partial(main_kernel, dims), out_shape=(jax.Shape...]
where the time goes in v4:
time: 55.9 us; the launch traced here: 55.7 us
  Pallas kernels  54.4 us (97%)
  between operations  0.7 us (1%)
  local copies, waits for them, and re-layouts  0.69 us (1%)
    pallas_call x1, Pallas kernels, body(): pl.pallas_call(functools.partial(main_kernel, dims), out_shape=(jax.Shape...  49.6 us
    pallas_call x1, Pallas kernels, body(): pl.pallas_call(functools.partial(fetch_kernel, dims), out_shape=jax.Shape...  3.13 us
    pallas_call x1, Pallas kernels, body(): pl.pallas_call(last_kernel, out_shape=(jax.ShapeDtypeStruct((fronts, shar...  1.64 us

profile of v4, /device:TPU:0, one launch (start us, length us, event | category | flops | bytes accessed | tf_op | source)
XLA Modules:
  0.0 55.7 jit_solution(9627522185746504868)
XLA Ops:
  0.6 0.0 copy-start.2
  0.6 0.7 %copy-done.2 = s32[2,16]{1,0:T(2,128)S(1)} copy-done((s32[2,16]{1,0:T(2,128)S(1)}, s32[2,16]{1,0:T(2,128)}, u32[]{:S(2)}) %copy-start.2) | copy-done | bytes 152
  1.3 0.0 copy-start
  1.3 0.0 copy-start.3
  1.3 0.0 copy-start.4
  1.3 3.1 %shard_map.68.tiles = f32[2,4,256,512]{3,2,1,0:T(8,128)S(1)} custom-call(s32[2,16]{1,0:T(2,128)S(1)} %copy-done.2, f32[4096,2048]{1,0:T(8,128)} %inv.1), custom_call_target="tpu_custom_call" | custom-call | tf_op jit(solution)/shard_map/pallas_call | solution.py:603
  4.5 0.0 copy-done
  4.5 0.0 copy-done.3
  4.5 0.0 copy-done.4
  4.5 0.0 copy-start.1
  4.5 49.6 %shard_map.69 = (f32[2,128,256]{2,1,0:T(8,128)S(1)}, f32[4,8,16,128]{3,2,1,0:T(8,128)S(1)}) custom-call(s32[2,16]{1,0:T(2,128)S(1)} %copy-done.3, s32[2,4]{1,0:T(2,128)S(1)} %copy-done.4, f32[2,4,256,512]{3,2,1,0:T(8,128)S(1)} %shard_map.68.tiles, f32[2,4,256,256]{3,2,1,0:T(8,128)S(1)} %bitcast.2), custom_call_target="tpu_custom_call" | custom-call | tf_op jit(solution)/shard_map/pallas_call | solution.py:618
  54.1 0.0 copy-done.1
  54.1 1.6 %shard_map.70 = (f32[2,128,256]{2,1,0:T(8,128)}, f32[2,256,256]{2,1,0:T(8,128)}) custom-call(s32[2,4]{1,0:T(2,128)S(1)} %copy-done.4, f32[2,128,256]{2,1,0:T(8,128)S(1)} %get-tuple-element.4.bsum, f32[4,128,128]{2,1,0:T(8,128)S(1)} %bitcast.3, f32[2,256,256]{2,1,0:T(8,128)S(1)} %copy-done.1), custom_call_target="tpu_custom_call" | custom-call | tf_op jit(solution)/shard_map/pallas_call | solution.py:678
Async XLA Ops:
  0.6 0.7 %copy-start.2 = (s32[2,16]{1,0:T(2,128)S(1)}, s32[2,16]{1,0:T(2,128)}, u32[]{:S(2)}) copy-start(s32[2,16]{1,0:T(2,128)} %fb_hbm.3) | copy-start | bytes 388
  1.3 3.1 %copy-start = (f32[2,1024,256]{2,1,0:T(8,128)S(1)}, f32[2,1024,256]{2,1,0:T(8,128)}, u32[]{:S(2)}) copy-start(f32[2,1024,256]{2,1,0:T(8,128)} %param.7) | copy-start | bytes 6291460
  1.3 3.2 %copy-start.3 = (s32[2,16]{1,0:T(2,128)S(1)}, s32[2,16]{1,0:T(2,128)}, u32[]{:S(2)}) copy-start(s32[2,16]{1,0:T(2,128)} %fb_hbm.3) | copy-start | bytes 388
  1.3 3.2 %copy-start.4 = (s32[2,4]{1,0:T(2,128)S(1)}, s32[2,4]{1,0:T(2,128)}, u32[]{:S(2)}) copy-start(s32[2,4]{1,0:T(2,128)} %bounds.1) | copy-start | bytes 100
  4.5 49.6 %copy-start.1 = (f32[2,256,256]{2,1,0:T(8,128)S(1)}, f32[2,256,256]{2,1,0:T(8,128)}, u32[]{:S(2)}) copy-start(f32[2,256,256]{2,1,0:T(8,128)} %terms.1) | copy-start | bytes 1572868

commit v5 on v4

--- a/solution.py
+++ b/solution.py
@@ -108,7 +108,7 @@
 
 
 def main_kernel(
-    dims, fb_hbm, bounds_hbm, tiles, panels, bsum, pkall,
+    dims, fb_hbm, bounds_hbm, tiles, panels, bsum, pkall, masks,
     fb, bounds, th, tl, bm, wb, part, xbuf, xs, rbuf, qs, zbuf, zs, pth, ptl,
     pfh, pfl, own_u, par_s, par_r, p0, zn, fs, zf, x0, x0r, rs0, rb0, q0, zc, inner0, tah, tal, tbh, tbl,
     dpk, csb, hs, rsb, zb, local_sem, send_sem, recv_sem,
@@ -227,6 +227,15 @@
             hi, lo = split(panels[f, j].T)
             pfh[f, j] = hi
             pfl[f, j] = lo
+
+    def mask_nodes():
+        for f in range(fronts):
+            for h in range(nh):
+                cols = node_ids(bounds, f, h * hw, (half, hw), 1)
+                for a in range(width // half):
+                    same = node_ids(bounds, f, a * half, (half, hw), 0) == cols
+                    at = (f, pl.ds(a * half, half), pl.ds(h * hw, hw))
+                    masks[at] = same.astype(jnp.float32)
 
     def split_first():
         upper = pl.ds(pl.multiple_of(s * share, share), sh2)
@@ -493,6 +502,7 @@
     w_relay(1)
     w_send(2)
     split_first()
+    mask_nodes()
 
     tasks = {}
 
@@ -559,17 +569,21 @@
     mail.close()
 
 
-def last_kernel(bounds, bsum, pk, terms, border, diag):
+def last_kernel(masks, bsum, pk, terms, border, diag, neg, full, sem):
     fronts, width = terms.shape[:2]
     half, hw = pk.shape[1:]
-    border[...] = -bsum[...]
+    neg[...] = -bsum[...]
+    copies = [pltpu.make_async_copy(neg, border, sem.at[fronts])]
+    copies[0].start()
     for f in range(fronts):
         for h in range(width // hw):
-            cols = node_ids(bounds, f, h * hw, (half, hw), 1)
             for a in range(width // half):
-                same = (node_ids(bounds, f, a * half, (half, hw), 0) == cols).astype(jnp.float32)
                 at = (f, pl.ds(a * half, half), pl.ds(h * hw, hw))
-                diag[at] = same * (terms[at] + pk[f * (width // hw) + h])
+                full[at] = masks[at] * (terms[at] + pk[f * (width // hw) + h])
+        copies.append(pltpu.make_async_copy(full.at[f], diag.at[f], sem.at[f]))
+        copies[-1].start()
+    for copy in copies:
+        copy.wait()
 
 
 def body(inverse, front_blocks, panels, diag_terms, bounds):
@@ -596,7 +610,6 @@
     dims = (fronts, kb, n_row, n_col, nz, nx, rg, cg, nh, hw)
     f32, bf16 = jnp.float32, jnp.bfloat16
     vmem = pl.BlockSpec(memory_space=pltpu.VMEM)
-    smem = pl.BlockSpec(memory_space=pltpu.SMEM)
     anywhere = pl.BlockSpec(memory_space=pltpu.HBM)
     blocks = panels.reshape(fronts, per_owner, BS, width)
 
@@ -615,14 +628,15 @@
 
     count = copies_of(dims)
     V = pltpu.VMEM
-    bsum, pk = pl.pallas_call(
+    bsum, pk, masks = pl.pallas_call(
         functools.partial(main_kernel, dims),
         out_shape=(
             jax.ShapeDtypeStruct((fronts, share, width), f32),
             jax.ShapeDtypeStruct((chunks, groups, rows_each, hw), f32),
+            jax.ShapeDtypeStruct((fronts, width, width), f32),
         ),
         in_specs=[anywhere, anywhere, vmem, vmem],
-        out_specs=(vmem, vmem),
+        out_specs=(vmem, vmem, vmem),
         scratch_shapes=[
             pltpu.SMEM((fronts, kb), jnp.int32),
             pltpu.SMEM(bounds.shape, jnp.int32),
@@ -681,10 +695,15 @@
             jax.ShapeDtypeStruct((fronts, share, width), f32),
             jax.ShapeDtypeStruct((fronts, width, width), f32),
         ),
-        in_specs=[smem, vmem, vmem, vmem],
-        out_specs=(vmem, vmem),
+        in_specs=[vmem, vmem, vmem, vmem],
+        out_specs=(anywhere, anywhere),
+        scratch_shapes=[
+            V((fronts, share, width), f32),
+            V((fronts, width, width), f32),
+            pltpu.SemaphoreType.DMA((fronts + 1,)),
+        ],
         compiler_params=pltpu.CompilerParams(vmem_limit_bytes=16 << 20),
-    )(bounds, bsum, pk.reshape(chunks, half, hw), diag_terms)
+    )(masks, bsum, pk.reshape(chunks, half, hw), diag_terms)
 
 
 def solution(mesh):

time: 55.9 us -> 55.3 us (0.989)
  Pallas kernels: 54.4 us -> 53.7 us
    pallas_call x1, Pallas kernels: 1.64 us -> 0.92 us  [body(): pl.pallas_call(last_kernel, out_shape=(jax.ShapeDtypeStruct((fronts, shar...]
where the time goes in v5:
time: 55.3 us; the launch traced here: 55.1 us
  Pallas kernels  53.7 us (97%)
  between operations  0.7 us (1%)
  local copies, waits for them, and re-layouts  0.69 us (1%)
    pallas_call x1, Pallas kernels, body(): pl.pallas_call(functools.partial(main_kernel, dims), out_shape=(jax.Shape...  49.7 us
    pallas_call x1, Pallas kernels, body(): pl.pallas_call(functools.partial(fetch_kernel, dims), out_shape=jax.Shape...  3.13 us

profile of v5, /device:TPU:0, one launch (start us, length us, event | category | flops | bytes accessed | tf_op | source)
XLA Modules:
  0.0 55.1 jit_solution(3623829222593717098)
XLA Ops:
  0.6 0.0 copy-start.2
  0.6 0.7 %copy-done.2 = s32[2,16]{1,0:T(2,128)S(1)} copy-done((s32[2,16]{1,0:T(2,128)S(1)}, s32[2,16]{1,0:T(2,128)}, u32[]{:S(2)}) %copy-start.2) | copy-done | bytes 152
  1.3 0.0 copy-start
  1.3 0.0 copy-start.3
  1.3 0.0 copy-start.4
  1.3 3.1 %shard_map.68.tiles = f32[2,4,256,512]{3,2,1,0:T(8,128)S(1)} custom-call(s32[2,16]{1,0:T(2,128)S(1)} %copy-done.2, f32[4096,2048]{1,0:T(8,128)} %inv.1), custom_call_target="tpu_custom_call" | custom-call | tf_op jit(solution)/shard_map/pallas_call | solution.py:616
  4.5 0.0 copy-done
  4.5 0.0 copy-done.3
  4.5 0.0 copy-done.4
  4.5 0.0 copy-start.1
  4.5 49.7 %shard_map.69 = (f32[2,128,256]{2,1,0:T(8,128)S(1)}, f32[4,8,16,128]{3,2,1,0:T(8,128)S(1)}, f32[2,256,256]{2,1,0:T(8,128)S(1)}) custom-call(s32[2,16]{1,0:T(2,128)S(1)} %copy-done.3, s32[2,4]{1,0:T(2,128)S(1)} %copy-done.4, f32[2,4,256,512]{3,2,1,0:T(8,128)S(1)} %shard_map.68.tiles, f32[2,4,256,256]{3,2,1,0:T(8,128)S(1)} %bitcast.2), custom_call_target="tpu_custom_call" | custom-call | tf_op jit(solution)/shard_map/pallas_call | solution.py:631
  54.2 0.0 copy-done.1
  54.2 0.9 %shard_map.70 = (f32[2,128,256]{2,1,0:T(8,128)}, f32[2,256,256]{2,1,0:T(8,128)}) custom-call(f32[2,256,256]{2,1,0:T(8,128)S(1)} %get-tuple-element.5.masks, f32[2,128,256]{2,1,0:T(8,128)S(1)} %get-tuple-element.6.bsum, f32[4,128,128]{2,1,0:T(8,128)S(1)} %bitcast.3, f32[2,256,256]{2,1,0:T(8,128)S(1)} %copy-done.1), custom_call_target="tpu_custom_call" | custom-call | tf_op jit(solution)/shard_map/pallas_call | solution.py:692
Async XLA Ops:
  0.6 0.7 %copy-start.2 = (s32[2,16]{1,0:T(2,128)S(1)}, s32[2,16]{1,0:T(2,128)}, u32[]{:S(2)}) copy-start(s32[2,16]{1,0:T(2,128)} %fb_hbm.3) | copy-start | bytes 388
  1.3 3.1 %copy-start = (f32[2,1024,256]{2,1,0:T(8,128)S(1)}, f32[2,1024,256]{2,1,0:T(8,128)}, u32[]{:S(2)}) copy-start(f32[2,1024,256]{2,1,0:T(8,128)} %param.7) | copy-start | bytes 6291460
  1.3 3.2 %copy-start.3 = (s32[2,16]{1,0:T(2,128)S(1)}, s32[2,16]{1,0:T(2,128)}, u32[]{:S(2)}) copy-start(s32[2,16]{1,0:T(2,128)} %fb_hbm.3) | copy-start | bytes 388
  1.3 3.2 %copy-start.4 = (s32[2,4]{1,0:T(2,128)S(1)}, s32[2,4]{1,0:T(2,128)}, u32[]{:S(2)}) copy-start(s32[2,4]{1,0:T(2,128)} %bounds_hbm.1) | copy-start | bytes 100
  4.5 49.7 %copy-start.1 = (f32[2,256,256]{2,1,0:T(8,128)S(1)}, f32[2,256,256]{2,1,0:T(8,128)}, u32[]{:S(2)}) copy-start(f32[2,256,256]{2,1,0:T(8,128)} %terms.1) | copy-start | bytes 1572868

commit v6 on v5

--- a/solution.py
+++ b/solution.py
@@ -552,10 +552,10 @@
     z_first(last, (1,))
     diag_sum(last)
     diag_back(1)
+    diag_back(2)
+    diag_back(0)
     z_second(last)
     z_first(last, (0,))
-    diag_back(2)
-    diag_back(0)
     diag_share(1)
     diag_back(last)
     diag_share(2)

time: 55.3 us -> 54.9 us (level)
  no operation moved by 1% of the time
where the time goes in v6:
time: 54.9 us; the launch traced here: 54.7 us
  Pallas kernels  53.3 us (97%)
  between operations  0.7 us (1%)
  local copies, waits for them, and re-layouts  0.69 us (1%)
    pallas_call x1, Pallas kernels, body(): pl.pallas_call(functools.partial(main_kernel, dims), out_shape=(jax.Shape...  49.3 us
    pallas_call x1, Pallas kernels, body(): pl.pallas_call(functools.partial(fetch_kernel, dims), out_shape=jax.Shape...  3.13 us

profile of v6, /device:TPU:0, one launch (start us, length us, event | category | flops | bytes accessed | tf_op | source)
XLA Modules:
  0.0 54.7 jit_solution(15531911712403816773)
XLA Ops:
  0.6 0.0 copy-start.2
  0.6 0.7 %copy-done.2 = s32[2,16]{1,0:T(2,128)S(1)} copy-done((s32[2,16]{1,0:T(2,128)S(1)}, s32[2,16]{1,0:T(2,128)}, u32[]{:S(2)}) %copy-start.2) | copy-done | bytes 152
  1.3 0.0 copy-start
  1.3 0.0 copy-start.3
  1.3 0.0 copy-start.4
  1.3 3.1 %shard_map.68.tiles = f32[2,4,256,512]{3,2,1,0:T(8,128)S(1)} custom-call(s32[2,16]{1,0:T(2,128)S(1)} %copy-done.2, f32[4096,2048]{1,0:T(8,128)} %inv.1), custom_call_target="tpu_custom_call" | custom-call | tf_op jit(solution)/shard_map/pallas_call | solution.py:616
  4.5 0.0 copy-done
  4.5 0.0 copy-done.3
  4.5 0.0 copy-done.4
  4.5 0.0 copy-start.1
  4.5 49.3 %shard_map.69 = (f32[2,128,256]{2,1,0:T(8,128)S(1)}, f32[4,8,16,128]{3,2,1,0:T(8,128)S(1)}, f32[2,256,256]{2,1,0:T(8,128)S(1)}) custom-call(s32[2,16]{1,0:T(2,128)S(1)} %copy-done.3, s32[2,4]{1,0:T(2,128)S(1)} %copy-done.4, f32[2,4,256,512]{3,2,1,0:T(8,128)S(1)} %shard_map.68.tiles, f32[2,4,256,256]{3,2,1,0:T(8,128)S(1)} %bitcast.2), custom_call_target="tpu_custom_call" | custom-call | tf_op jit(solution)/shard_map/pallas_call | solution.py:631
  53.8 0.0 copy-done.1
  53.8 0.9 %shard_map.70 = (f32[2,128,256]{2,1,0:T(8,128)}, f32[2,256,256]{2,1,0:T(8,128)}) custom-call(f32[2,256,256]{2,1,0:T(8,128)S(1)} %get-tuple-element.5.masks, f32[2,128,256]{2,1,0:T(8,128)S(1)} %get-tuple-element.6.bsum, f32[4,128,128]{2,1,0:T(8,128)S(1)} %bitcast.3, f32[2,256,256]{2,1,0:T(8,128)S(1)} %copy-done.1), custom_call_target="tpu_custom_call" | custom-call | tf_op jit(solution)/shard_map/pallas_call | solution.py:692
Async XLA Ops:
  0.6 0.7 %copy-start.2 = (s32[2,16]{1,0:T(2,128)S(1)}, s32[2,16]{1,0:T(2,128)}, u32[]{:S(2)}) copy-start(s32[2,16]{1,0:T(2,128)} %fb_hbm.3) | copy-start | bytes 388
  1.3 3.1 %copy-start = (f32[2,1024,256]{2,1,0:T(8,128)S(1)}, f32[2,1024,256]{2,1,0:T(8,128)}, u32[]{:S(2)}) copy-start(f32[2,1024,256]{2,1,0:T(8,128)} %param.7) | copy-start | bytes 6291460
  1.3 3.2 %copy-start.3 = (s32[2,16]{1,0:T(2,128)S(1)}, s32[2,16]{1,0:T(2,128)}, u32[]{:S(2)}) copy-start(s32[2,16]{1,0:T(2,128)} %fb_hbm.3) | copy-start | bytes 388
  1.3 3.2 %copy-start.4 = (s32[2,4]{1,0:T(2,128)S(1)}, s32[2,4]{1,0:T(2,128)}, u32[]{:S(2)}) copy-start(s32[2,4]{1,0:T(2,128)} %bounds_hbm.1) | copy-start | bytes 100
  4.5 49.3 %copy-start.1 = (f32[2,256,256]{2,1,0:T(8,128)S(1)}, f32[2,256,256]{2,1,0:T(8,128)}, u32[]{:S(2)}) copy-start(f32[2,256,256]{2,1,0:T(8,128)} %terms.1) | copy-start | bytes 1572868

commit v7 on v6

--- a/solution.py
+++ b/solution.py
@@ -34,21 +34,22 @@
     for f in range(fronts):
         cols = [jnp.int32(0)] * nc
         m = jnp.int32(0)
-        rows = [jnp.int32(0)] * n_row
         for p in range(kb):
             b = fb[f, p]
             there = b // cg == c
             for k in range(nc):
                 cols[k] = jnp.where(there & (m == k), b % cg, cols[k])
             m = m + there.astype(jnp.int32)
-            t = p // per_owner
-            rows[t] = jnp.where(b // rg == r, b % rg, rows[t])
         for t in range(n_row):
+            row = jnp.int32(0)
+            for p in range(t * per_owner, (t + 1) * per_owner):
+                b = fb[f, p]
+                row = jnp.where(b // rg == r, b % rg, row)
             for k in range(nc):
                 copies.append(
                     pltpu.make_async_copy(
                         inv.at[
-                            pl.ds(pl.multiple_of(rows[t] * BS, BS), BS),
+                            pl.ds(pl.multiple_of(row * BS, BS), BS),
                             pl.ds(pl.multiple_of(cols[k] * BS, BS), BS),
                         ],
                         tiles.at[f, t, :, pl.ds(k * BS, BS)],

time: 54.9 us -> 54.9 us (level)
  no operation moved by 1% of the time
where the time goes in v7:
time: 54.9 us; the launch traced here: 54.8 us
  Pallas kernels  53.4 us (97%)
  between operations  0.7 us (1%)
  local copies, waits for them, and re-layouts  0.69 us (1%)
    pallas_call x1, Pallas kernels, body(): pl.pallas_call(functools.partial(main_kernel, dims), out_shape=(jax.Shape...  49.3 us
    pallas_call x1, Pallas kernels, body(): pl.pallas_call(functools.partial(fetch_kernel, dims), out_shape=jax.Shape...  3.15 us

profile of v7, /device:TPU:0, one launch (start us, length us, event | category | flops | bytes accessed | tf_op | source)
XLA Modules:
  0.0 54.8 jit_solution(6377579772775770203)
XLA Ops:
  0.6 0.0 copy-start.2
  0.6 0.7 %copy-done.2 = s32[2,16]{1,0:T(2,128)S(1)} copy-done((s32[2,16]{1,0:T(2,128)S(1)}, s32[2,16]{1,0:T(2,128)}, u32[]{:S(2)}) %copy-start.2) | copy-done | bytes 152
  1.3 0.0 copy-start
  1.3 0.0 copy-start.3
  1.3 0.0 copy-start.4
  1.3 3.2 %shard_map.68.tiles = f32[2,4,256,512]{3,2,1,0:T(8,128)S(1)} custom-call(s32[2,16]{1,0:T(2,128)S(1)} %copy-done.2, f32[4096,2048]{1,0:T(8,128)} %inv.1), custom_call_target="tpu_custom_call" | custom-call | tf_op jit(solution)/shard_map/pallas_call | solution.py:617
  4.5 0.0 copy-done
  4.5 0.0 copy-done.3
  4.5 0.0 copy-done.4
  4.5 0.0 copy-start.1
  4.5 49.3 %shard_map.69 = (f32[2,128,256]{2,1,0:T(8,128)S(1)}, f32[4,8,16,128]{3,2,1,0:T(8,128)S(1)}, f32[2,256,256]{2,1,0:T(8,128)S(1)}) custom-call(s32[2,16]{1,0:T(2,128)S(1)} %copy-done.3, s32[2,4]{1,0:T(2,128)S(1)} %copy-done.4, f32[2,4,256,512]{3,2,1,0:T(8,128)S(1)} %shard_map.68.tiles, f32[2,4,256,256]{3,2,1,0:T(8,128)S(1)} %bitcast.2), custom_call_target="tpu_custom_call" | custom-call | tf_op jit(solution)/shard_map/pallas_call | solution.py:632
  53.8 0.0 copy-done.1
  53.8 0.9 %shard_map.70 = (f32[2,128,256]{2,1,0:T(8,128)}, f32[2,256,256]{2,1,0:T(8,128)}) custom-call(f32[2,256,256]{2,1,0:T(8,128)S(1)} %get-tuple-element.5.masks, f32[2,128,256]{2,1,0:T(8,128)S(1)} %get-tuple-element.6.bsum, f32[4,128,128]{2,1,0:T(8,128)S(1)} %bitcast.3, f32[2,256,256]{2,1,0:T(8,128)S(1)} %copy-done.1), custom_call_target="tpu_custom_call" | custom-call | tf_op jit(solution)/shard_map/pallas_call | solution.py:693
Async XLA Ops:
  0.6 0.7 %copy-start.2 = (s32[2,16]{1,0:T(2,128)S(1)}, s32[2,16]{1,0:T(2,128)}, u32[]{:S(2)}) copy-start(s32[2,16]{1,0:T(2,128)} %fb_hbm.3) | copy-start | bytes 388
  1.3 3.2 %copy-start = (f32[2,1024,256]{2,1,0:T(8,128)S(1)}, f32[2,1024,256]{2,1,0:T(8,128)}, u32[]{:S(2)}) copy-start(f32[2,1024,256]{2,1,0:T(8,128)} %param.7) | copy-start | bytes 6291460
  1.3 3.2 %copy-start.3 = (s32[2,16]{1,0:T(2,128)S(1)}, s32[2,16]{1,0:T(2,128)}, u32[]{:S(2)}) copy-start(s32[2,16]{1,0:T(2,128)} %fb_hbm.3) | copy-start | bytes 388
  1.3 3.2 %copy-start.4 = (s32[2,4]{1,0:T(2,128)S(1)}, s32[2,4]{1,0:T(2,128)}, u32[]{:S(2)}) copy-start(s32[2,4]{1,0:T(2,128)} %bounds_hbm.1) | copy-start | bytes 100
  4.5 49.3 %copy-start.1 = (f32[2,256,256]{2,1,0:T(8,128)S(1)}, f32[2,256,256]{2,1,0:T(8,128)}, u32[]{:S(2)}) copy-start(f32[2,256,256]{2,1,0:T(8,128)} %terms.1) | copy-start | bytes 1572868
